TPU v7x, 128 devices: a whole 4x4x4 slice. The times are simulated.
128 devices in a mesh: row: 8 (over x, z_hi), col: 16 (over z_lo, y, core).
Axes of the slice: x: 4, y: 4, z: 4 (z_hi: 2, z_lo: 2; z = z_hi * 2 + z_lo), core: 2. Of those that a mesh axis runs over, the one named last changes fastest.
Arguments:
- blocks: float32 [2048, 16, 1024], P(('row', 'col')), may hold values from -2 to 2
- columns: int32 [1024, 16], replicated, may hold values from 0 to 1023, as said below
- owner_slot: int32 [1024], replicated, may hold values from 0 to 2047, as said below
- keep_mask: int32 [1024, 16], P('row', 'col'), may hold values 0 or 1
Outputs:
- filtered: float32 [1024, 16, 1024], P('row', 'col')
- trace_mean: float32 [], replicated
Inputs may be any that keep to these rules, and one draw needn't show every extreme that they name: `columns`: slot g of block row i holds column g * 64 + (i % 64 + o) % 64 for some 0 <= o < 64; in the group g = i // 64 it is i itself. Every block row has its own slot; owner_slot[i] = d * 16 + (i // 64) + r with owner d and r < 1; for every column group some owner fills all 1 of its slots.
All inputs are finite; a program needn't handle non-finite values. No bound on the sum of `keep_mask` on one device may be relied on, other than what follows from the above.
Results may differ from a plain program's by a relative error of at most 0.0003.
Values sent between devices are 32-bit elements; how exact they have to be, the bound alone decides.
A program may use at most 64 MiB of HBM per device.

v0:
```python
import jax
import jax.numpy as jnp
from jax import lax
from jax.sharding import PartitionSpec as P

BS = 32


HIGHEST = lax.Precision.HIGHEST


def shifted(block, axis, distance):
    devices = range(lax.axis_size(axis))
    route = [((i - distance) % len(devices), i) for i in devices]
    return lax.ppermute(block, axis, route)


def step_product(
    totals, left_panel, right_panel, columns, panel_first, result_columns, group_index, column_index
):
    panel_rows = left_panel.shape[0]
    group_rows = right_panel.shape[0]
    per_group = result_columns.shape[1]
    inner_columns = lax.dynamic_slice(
        columns, (panel_first, group_index * per_group), (panel_rows, per_group)
    )
    local_rows = inner_columns - group_index * group_rows
    far_columns = lax.dynamic_slice_in_dim(columns, column_index * per_group, per_group, 1)[
        inner_columns
    ]
    matches = (far_columns[:, :, None, :] == result_columns[:, None, :, None]).astype(jnp.float32)
    chosen = right_panel[local_rows].reshape(panel_rows, per_group, per_group, BS, BS)
    routed = jnp.einsum("racb,rabxy->racxy", matches, chosen, precision=HIGHEST)
    left_blocks = left_panel.reshape(panel_rows, per_group, BS, BS)
    return totals + jnp.einsum("raxz,raczy->rcxy", left_blocks, routed, precision=HIGHEST)


def shards(blocks, columns, owner_slot, keep_mask):
    row_count = lax.axis_size("row")
    col_count = lax.axis_size("col")
    row_index = lax.axis_index("row")
    column_index = lax.axis_index("col")
    owners = row_count * col_count
    total_rows, slot_count = columns.shape
    per_group = slot_count // col_count
    panel_rows = total_rows // row_count
    group_rows = total_rows // col_count
    halves = col_count // row_count
    owned_slots = blocks.shape[0]
    slot_depth = owned_slots // col_count
    block_area = blocks.shape[2]
    flat_width = per_group * block_area
    source = blocks.reshape(col_count, slot_depth, col_count, flat_width).transpose(0, 2, 1, 3)
    dest_rows = jnp.arange(row_count, dtype=jnp.int32)[:, None, None]
    dest_cols = jnp.arange(col_count, dtype=jnp.int32)[None, :, None]
    member = jnp.arange(halves, dtype=jnp.int32)[None, None, :]
    send_left = source[dest_rows * halves + member, (dest_rows + dest_cols) % col_count]
    send_right = source[(dest_rows + dest_cols) % row_count + member * row_count, dest_cols]
    outgoing = jnp.stack([send_left, send_right], axis=2)
    arrived = lax.all_to_all(
        outgoing.reshape(owners, 2 * halves * slot_depth, flat_width),
        ("row", "col"),
        split_axis=0,
        concat_axis=0,
        tiled=True,
    )
    arrived = arrived.reshape(owners, 2, halves * slot_depth, flat_width)
    from_left = arrived[:, 0].reshape(owners * halves * slot_depth, flat_width)
    from_right = arrived[:, 1].reshape(owners * halves * slot_depth, flat_width)
    panel_first = row_index * panel_rows
    panel_ids = panel_first + jnp.arange(panel_rows, dtype=jnp.int32)
    panel_slots = lax.dynamic_slice_in_dim(owner_slot, panel_first, panel_rows)
    bucket = panel_ids // group_rows
    position = (
        (panel_slots // owned_slots * halves + bucket - row_index * halves) * slot_depth
        + panel_slots % owned_slots
        - bucket * slot_depth
    )
    left_panel = from_left[position]
    first_bucket = (row_index + column_index) % row_count
    member_ids = jnp.arange(halves, dtype=jnp.int32)
    right_buckets = first_bucket + member_ids * row_count
    right_rows = (
        right_buckets[:, None] * group_rows + jnp.arange(group_rows, dtype=jnp.int32)[None, :]
    )
    right_slots = owner_slot[right_rows]
    right_position = (
        (right_slots // owned_slots * halves + member_ids[:, None]) * slot_depth
        + right_slots % owned_slots
        - right_buckets[:, None] * slot_depth
    )
    right_pair = from_right[right_position]
    result_columns = lax.dynamic_slice(
        columns, (panel_first, column_index * per_group), (panel_rows, per_group)
    )

    def pick_right(right_now, group_index):
        return right_now[group_index // row_count]

    def advance(step_index, carry):
        totals, left_now, right_now = carry
        group_index = (row_index + column_index + step_index) % col_count
        right_panel = pick_right(right_now, group_index)
        totals = step_product(
            totals,
            left_now,
            right_panel,
            columns,
            panel_first,
            result_columns,
            group_index,
            column_index,
        )
        left_next = shifted(left_now, "col", -1)
        right_next = shifted(right_now, "row", -1)
        return (totals, left_next, right_next)

    zeros = jnp.zeros((panel_rows, per_group, BS, BS), jnp.float32)
    totals, left_last, right_last = lax.fori_loop(
        0, col_count - 1, advance, (zeros, left_panel, right_pair)
    )
    last_step = col_count - 1
    last_group = (row_index + column_index + last_step) % col_count
    totals = step_product(
        totals,
        left_last,
        pick_right(right_last, last_group),
        columns,
        panel_first,
        result_columns,
        last_group,
        column_index,
    )
    diagonal = (result_columns == panel_ids[:, None]).astype(jnp.float32)
    traces = jnp.trace(totals, axis1=2, axis2=3)
    total_trace = lax.psum(jnp.sum(diagonal * traces), ("row", "col"))
    trace_mean = total_trace / total_rows
    filtered = (totals * keep_mask[:, :, None, None].astype(jnp.float32)).reshape(
        panel_rows, per_group, block_area
    )
    return (filtered, trace_mean)


def solution(mesh):
    in_specs = (P(("row", "col"), None, None), P(), P(), P("row", "col"))
    out_specs = (P("row", "col", None), P())
    return jax.shard_map(shards, mesh=mesh, in_specs=in_specs, out_specs=out_specs, check_vma=False)
```

profile of v0, /device:TPU:1, one launch (start us, length us, event | category | flops | bytes accessed | tf_op | source)
XLA Modules:
  0.0 534.5 jit_solution(13668569332533858415)
XLA Ops:
  13.9 11.5 %all-to-all-start = ((f32[128,4,1024]{2,1,0:T(4,128)}), f32[128,4,1024]{2,1,0:T(4,128)S(1)}, u32[]{:S(2)}, u32[]{:S(2)}) async-start(f32[128,4,1024]{2,1,0:T(4,128)} %copy.26), calls=%async_computation | async-start | bytes 4194304 | tf_op jit(solution)/shard_map/all_to_all | solution.py:60
  30.3 25.3 %all-to-all-done = f32[128,4,1024]{2,1,0:T(4,128)S(1)} async-done(((f32[128,4,1024]{2,1,0:T(4,128)}), f32[128,4,1024]{2,1,0:T(4,128)S(1)}, u32[]{:S(2)}, u32[]{:S(2)}) %all-to-all-start) | async-done | bytes 2097184 | tf_op jit(solution)/shard_map/all_to_all | solution.py:60
  69.6 375.6 %while.20 = (s32[]{:T(128)}, f32[128,1,32,32]{2,3,0,1:T(8,128)}, f32[128,1024]{0,1:T(8,128)}, f32[2,64,1024]{2,1,0:T(8,128)}, s32[]{:T(128)}, /*index=5*/s32[102...) while((s32[]{:T(128)}, f32[128,1,32,32]{2,3,0,1:T(8,128)}, ...), condition=%wide.region_1.2_spmd.clone, body=%wide.region_0.1_spmd.clone.sunk | while | flops 50728100 | bytes 14171237 | solution.py:119
  86.0 6.4 %bitcast_add_fusion.3 = f32[128,1,32,32]{2,3,0,1:T(8,128)} fusion(f32[128,1,32,32]{2,3,0,1:T(8,128)} %get-tuple-element.410, f32[128,32,32]{1,2,0:T(8,128)S(1)} %copy.40, f32[128,32,32]{2,1,0:T(8,128)} %copy.41, pred[]{:T(512)S(6)} %compare.42), kind=kOutput, calls=%fused_computation.9.clone.1 | convolution fusion | flops 50593792 | bytes 2097153 | tf_op jit(solution)/shard_map/while/body/eval_jaxpr/raxz,raczy->rcxy/dot_general | solution.py:35
  111.2 7.0 %bitcast_add_fusion.3 = f32[128,1,32,32]{2,3,0,1:T(8,128)} fusion(f32[128,1,32,32]{2,3,0,1:T(8,128)} %get-tuple-element.410, f32[128,32,32]{1,2,0:T(8,128)S(1)} %copy.40, f32[128,32,32]{2,1,0:T(8,128)} %copy.41, pred[]{:T(512)S(6)} %compare.42), kind=kOutput, calls=%fused_computation.9.clone.1 | convolution fusion | flops 50593792 | bytes 2097153 | tf_op jit(solution)/shard_map/while/body/eval_jaxpr/raxz,raczy->rcxy/dot_general | solution.py:35
  132.7 3.8 copy.41
  136.5 7.0 %bitcast_add_fusion.3 = f32[128,1,32,32]{2,3,0,1:T(8,128)} fusion(f32[128,1,32,32]{2,3,0,1:T(8,128)} %get-tuple-element.410, f32[128,32,32]{1,2,0:T(8,128)S(1)} %copy.40, f32[128,32,32]{2,1,0:T(8,128)} %copy.41, pred[]{:T(512)S(6)} %compare.42), kind=kOutput, calls=%fused_computation.9.clone.1 | convolution fusion | flops 50593792 | bytes 2097153 | tf_op jit(solution)/shard_map/while/body/eval_jaxpr/raxz,raczy->rcxy/dot_general | solution.py:35
  157.0 3.8 copy.41
  160.8 7.0 %bitcast_add_fusion.3 = f32[128,1,32,32]{2,3,0,1:T(8,128)} fusion(f32[128,1,32,32]{2,3,0,1:T(8,128)} %get-tuple-element.410, f32[128,32,32]{1,2,0:T(8,128)S(1)} %copy.40, f32[128,32,32]{2,1,0:T(8,128)} %copy.41, pred[]{:T(512)S(6)} %compare.42), kind=kOutput, calls=%fused_computation.9.clone.1 | convolution fusion | flops 50593792 | bytes 2097153 | tf_op jit(solution)/shard_map/while/body/eval_jaxpr/raxz,raczy->rcxy/dot_general | solution.py:35
  186.0 7.0 %bitcast_add_fusion.3 = f32[128,1,32,32]{2,3,0,1:T(8,128)} fusion(f32[128,1,32,32]{2,3,0,1:T(8,128)} %get-tuple-element.410, f32[128,32,32]{1,2,0:T(8,128)S(1)} %copy.40, f32[128,32,32]{2,1,0:T(8,128)} %copy.41, pred[]{:T(512)S(6)} %compare.42), kind=kOutput, calls=%fused_computation.9.clone.1 | convolution fusion | flops 50593792 | bytes 2097153 | tf_op jit(solution)/shard_map/while/body/eval_jaxpr/raxz,raczy->rcxy/dot_general | solution.py:35
  211.2 7.0 %bitcast_add_fusion.3 = f32[128,1,32,32]{2,3,0,1:T(8,128)} fusion(f32[128,1,32,32]{2,3,0,1:T(8,128)} %get-tuple-element.410, f32[128,32,32]{1,2,0:T(8,128)S(1)} %copy.40, f32[128,32,32]{2,1,0:T(8,128)} %copy.41, pred[]{:T(512)S(6)} %compare.42), kind=kOutput, calls=%fused_computation.9.clone.1 | convolution fusion | flops 50593792 | bytes 2097153 | tf_op jit(solution)/shard_map/while/body/eval_jaxpr/raxz,raczy->rcxy/dot_general | solution.py:35
  236.5 7.0 %bitcast_add_fusion.3 = f32[128,1,32,32]{2,3,0,1:T(8,128)} fusion(f32[128,1,32,32]{2,3,0,1:T(8,128)} %get-tuple-element.410, f32[128,32,32]{1,2,0:T(8,128)S(1)} %copy.40, f32[128,32,32]{2,1,0:T(8,128)} %copy.41, pred[]{:T(512)S(6)} %compare.42), kind=kOutput, calls=%fused_computation.9.clone.1 | convolution fusion | flops 50593792 | bytes 2097153 | tf_op jit(solution)/shard_map/while/body/eval_jaxpr/raxz,raczy->rcxy/dot_general | solution.py:35
  261.7 7.0 %bitcast_add_fusion.3 = f32[128,1,32,32]{2,3,0,1:T(8,128)} fusion(f32[128,1,32,32]{2,3,0,1:T(8,128)} %get-tuple-element.410, f32[128,32,32]{1,2,0:T(8,128)S(1)} %copy.40, f32[128,32,32]{2,1,0:T(8,128)} %copy.41, pred[]{:T(512)S(6)} %compare.42), kind=kOutput, calls=%fused_computation.9.clone.1 | convolution fusion | flops 50593792 | bytes 2097153 | tf_op jit(solution)/shard_map/while/body/eval_jaxpr/raxz,raczy->rcxy/dot_general | solution.py:35
  286.9 7.0 %bitcast_add_fusion.3 = f32[128,1,32,32]{2,3,0,1:T(8,128)} fusion(f32[128,1,32,32]{2,3,0,1:T(8,128)} %get-tuple-element.410, f32[128,32,32]{1,2,0:T(8,128)S(1)} %copy.40, f32[128,32,32]{2,1,0:T(8,128)} %copy.41, pred[]{:T(512)S(6)} %compare.42), kind=kOutput, calls=%fused_computation.9.clone.1 | convolution fusion | flops 50593792 | bytes 2097153 | tf_op jit(solution)/shard_map/while/body/eval_jaxpr/raxz,raczy->rcxy/dot_general | solution.py:35
  308.3 3.8 copy.41
  312.1 7.0 %bitcast_add_fusion.3 = f32[128,1,32,32]{2,3,0,1:T(8,128)} fusion(f32[128,1,32,32]{2,3,0,1:T(8,128)} %get-tuple-element.410, f32[128,32,32]{1,2,0:T(8,128)S(1)} %copy.40, f32[128,32,32]{2,1,0:T(8,128)} %copy.41, pred[]{:T(512)S(6)} %compare.42), kind=kOutput, calls=%fused_computation.9.clone.1 | convolution fusion | flops 50593792 | bytes 2097153 | tf_op jit(solution)/shard_map/while/body/eval_jaxpr/raxz,raczy->rcxy/dot_general | solution.py:35
  337.3 7.0 %bitcast_add_fusion.3 = f32[128,1,32,32]{2,3,0,1:T(8,128)} fusion(f32[128,1,32,32]{2,3,0,1:T(8,128)} %get-tuple-element.410, f32[128,32,32]{1,2,0:T(8,128)S(1)} %copy.40, f32[128,32,32]{2,1,0:T(8,128)} %copy.41, pred[]{:T(512)S(6)} %compare.42), kind=kOutput, calls=%fused_computation.9.clone.1 | convolution fusion | flops 50593792 | bytes 2097153 | tf_op jit(solution)/shard_map/while/body/eval_jaxpr/raxz,raczy->rcxy/dot_general | solution.py:35
  362.5 7.0 %bitcast_add_fusion.3 = f32[128,1,32,32]{2,3,0,1:T(8,128)} fusion(f32[128,1,32,32]{2,3,0,1:T(8,128)} %get-tuple-element.410, f32[128,32,32]{1,2,0:T(8,128)S(1)} %copy.40, f32[128,32,32]{2,1,0:T(8,128)} %copy.41, pred[]{:T(512)S(6)} %compare.42), kind=kOutput, calls=%fused_computation.9.clone.1 | convolution fusion | flops 50593792 | bytes 2097153 | tf_op jit(solution)/shard_map/while/body/eval_jaxpr/raxz,raczy->rcxy/dot_general | solution.py:35
  387.8 7.0 %bitcast_add_fusion.3 = f32[128,1,32,32]{2,3,0,1:T(8,128)} fusion(f32[128,1,32,32]{2,3,0,1:T(8,128)} %get-tuple-element.410, f32[128,32,32]{1,2,0:T(8,128)S(1)} %copy.40, f32[128,32,32]{2,1,0:T(8,128)} %copy.41, pred[]{:T(512)S(6)} %compare.42), kind=kOutput, calls=%fused_computation.9.clone.1 | convolution fusion | flops 50593792 | bytes 2097153 | tf_op jit(solution)/shard_map/while/body/eval_jaxpr/raxz,raczy->rcxy/dot_general | solution.py:35
  413.0 7.0 %bitcast_add_fusion.3 = f32[128,1,32,32]{2,3,0,1:T(8,128)} fusion(f32[128,1,32,32]{2,3,0,1:T(8,128)} %get-tuple-element.410, f32[128,32,32]{1,2,0:T(8,128)S(1)} %copy.40, f32[128,32,32]{2,1,0:T(8,128)} %copy.41, pred[]{:T(512)S(6)} %compare.42), kind=kOutput, calls=%fused_computation.9.clone.1 | convolution fusion | flops 50593792 | bytes 2097153 | tf_op jit(solution)/shard_map/while/body/eval_jaxpr/raxz,raczy->rcxy/dot_general | solution.py:35
  438.2 7.0 %bitcast_add_fusion.3 = f32[128,1,32,32]{2,3,0,1:T(8,128)} fusion(f32[128,1,32,32]{2,3,0,1:T(8,128)} %get-tuple-element.410, f32[128,32,32]{1,2,0:T(8,128)S(1)} %copy.40, f32[128,32,32]{2,1,0:T(8,128)} %copy.41, pred[]{:T(512)S(6)} %compare.42), kind=kOutput, calls=%fused_computation.9.clone.1 | convolution fusion | flops 50593792 | bytes 2097153 | tf_op jit(solution)/shard_map/while/body/eval_jaxpr/raxz,raczy->rcxy/dot_general | solution.py:35
  448.1 4.0 copy.32
  455.9 7.5 %select_reduce_fusion = (f32[128]{0:T(128)S(1)}, f32[128,1,32,32]{2,3,0,1:T(8,128)}) fusion(pred[32,32]{0,1:T(8,128)(4,1)S(1)} %iota_compare_fusion, f32[128]{0:T(128)S(1)} %convert_bitcast_fusion, f32[128,1,32,32]{2,3,0,1:T(8,128)S(1)} %copy-done.2, f32[128,32,32]{1,2,0:T(8,128)} %copy.32, f32[128,32,32]{2,1,0:T(8,128)} %copy.33), kind=kOutput, calls=%fused_computation.21 | convolution fusion | flops 50855808 | bytes 2099200 | tf_op jit(solution)/shard_map/raxz,raczy->rcxy/dot_general | solution.py:35
  464.0 64.8 %psum.7 = f32[]{:T(128)} all-reduce(f32[]{:T(128)} %fusion.19), channel_id=1, replica_groups=mesh['row'=8,'col'=16] {'row','col'}, use_global_device_ids=true, to_apply=%region_4.5 | all-reduce | flops 1 | bytes 8 | tf_op jit(solution)/shard_map/psum | solution.py:136
  (300 shorter events, 301.8 us)
Async XLA Ops:
  13.9 41.7 %all-to-all-start = ((f32[128,4,1024]{2,1,0:T(4,128)}), f32[128,4,1024]{2,1,0:T(4,128)S(1)}, u32[]{:S(2)}, u32[]{:S(2)}) async-start(f32[128,4,1024]{2,1,0:T(4,128)} %copy.26), calls=%async_computation | async-start | bytes 4194304 | tf_op jit(solution)/shard_map/all_to_all | solution.py:60
  71.5 20.9 %collective-permute-start = (f32[128,1024]{0,1:T(8,128)}, f32[128,1024]{0,1:T(8,128)}, u32[]{:S(2)}, u32[]{:S(2)}) collective-permute-start(f32[128,1024]{0,1:T(8,128)} %copy.48), channel_id=1, source_target_pairs={{1,0},{2,1},{3,2},{4,3},{5,4},{6,5},{7,6},{8,7},{9,8},{10,9},{11,1... | collective-permute-start | bytes 1572872 | tf_op jit(solution)/shard_map/while/body/eval_jaxpr/ppermute | solution.py:15
  94.3 23.9 %collective-permute-start = (f32[128,1024]{0,1:T(8,128)}, f32[128,1024]{0,1:T(8,128)}, u32[]{:S(2)}, u32[]{:S(2)}) collective-permute-start(f32[128,1024]{0,1:T(8,128)} %copy.48), channel_id=1, source_target_pairs={{1,0},{2,1},{3,2},{4,3},{5,4},{6,5},{7,6},{8,7},{9,8},{10,9},{11,1... | collective-permute-start | bytes 1572872 | tf_op jit(solution)/shard_map/while/body/eval_jaxpr/ppermute | solution.py:15
  98.3 19.9 %collective-permute-start.1 = (f32[2,64,1024]{2,1,0:T(8,128)}, f32[2,64,1024]{2,1,0:T(8,128)}, u32[]{:S(2)}, u32[]{:S(2)}) collective-permute-start(f32[2,64,1024]{2,1,0:T(8,128)} %copy.49), channel_id=1, source_target_pairs={{16,0},{32,16},{48,32},{64,48},{80,64},{96,80},{112,96},{0,112},{1... | collective-permute-start | bytes 1572872 | tf_op jit(solution)/shard_map/while/body/eval_jaxpr/ppermute | solution.py:15
  120.1 23.4 %collective-permute-start = (f32[128,1024]{0,1:T(8,128)}, f32[128,1024]{0,1:T(8,128)}, u32[]{:S(2)}, u32[]{:S(2)}) collective-permute-start(f32[128,1024]{0,1:T(8,128)} %copy.48), channel_id=1, source_target_pairs={{1,0},{2,1},{3,2},{4,3},{5,4},{6,5},{7,6},{8,7},{9,8},{10,9},{11,1... | collective-permute-start | bytes 1572872 | tf_op jit(solution)/shard_map/while/body/eval_jaxpr/ppermute | solution.py:15
  124.5 19.0 %collective-permute-start.1 = (f32[2,64,1024]{2,1,0:T(8,128)}, f32[2,64,1024]{2,1,0:T(8,128)}, u32[]{:S(2)}, u32[]{:S(2)}) collective-permute-start(f32[2,64,1024]{2,1,0:T(8,128)} %copy.49), channel_id=1, source_target_pairs={{16,0},{32,16},{48,32},{64,48},{80,64},{96,80},{112,96},{0,112},{1... | collective-permute-start | bytes 1572872 | tf_op jit(solution)/shard_map/while/body/eval_jaxpr/ppermute | solution.py:15
  145.4 22.4 %collective-permute-start = (f32[128,1024]{0,1:T(8,128)}, f32[128,1024]{0,1:T(8,128)}, u32[]{:S(2)}, u32[]{:S(2)}) collective-permute-start(f32[128,1024]{0,1:T(8,128)} %copy.48), channel_id=1, source_target_pairs={{1,0},{2,1},{3,2},{4,3},{5,4},{6,5},{7,6},{8,7},{9,8},{10,9},{11,1... | collective-permute-start | bytes 1572872 | tf_op jit(solution)/shard_map/while/body/eval_jaxpr/ppermute | solution.py:15
  149.3 18.5 %collective-permute-start.1 = (f32[2,64,1024]{2,1,0:T(8,128)}, f32[2,64,1024]{2,1,0:T(8,128)}, u32[]{:S(2)}, u32[]{:S(2)}) collective-permute-start(f32[2,64,1024]{2,1,0:T(8,128)} %copy.49), channel_id=1, source_target_pairs={{16,0},{32,16},{48,32},{64,48},{80,64},{96,80},{112,96},{0,112},{1... | collective-permute-start | bytes 1572872 | tf_op jit(solution)/shard_map/while/body/eval_jaxpr/ppermute | solution.py:15
  169.7 23.3 %collective-permute-start = (f32[128,1024]{0,1:T(8,128)}, f32[128,1024]{0,1:T(8,128)}, u32[]{:S(2)}, u32[]{:S(2)}) collective-permute-start(f32[128,1024]{0,1:T(8,128)} %copy.48), channel_id=1, source_target_pairs={{1,0},{2,1},{3,2},{4,3},{5,4},{6,5},{7,6},{8,7},{9,8},{10,9},{11,1... | collective-permute-start | bytes 1572872 | tf_op jit(solution)/shard_map/while/body/eval_jaxpr/ppermute | solution.py:15
  194.9 23.3 %collective-permute-start = (f32[128,1024]{0,1:T(8,128)}, f32[128,1024]{0,1:T(8,128)}, u32[]{:S(2)}, u32[]{:S(2)}) collective-permute-start(f32[128,1024]{0,1:T(8,128)} %copy.48), channel_id=1, source_target_pairs={{1,0},{2,1},{3,2},{4,3},{5,4},{6,5},{7,6},{8,7},{9,8},{10,9},{11,1... | collective-permute-start | bytes 1572872 | tf_op jit(solution)/shard_map/while/body/eval_jaxpr/ppermute | solution.py:15
  199.8 18.5 %collective-permute-start.1 = (f32[2,64,1024]{2,1,0:T(8,128)}, f32[2,64,1024]{2,1,0:T(8,128)}, u32[]{:S(2)}, u32[]{:S(2)}) collective-permute-start(f32[2,64,1024]{2,1,0:T(8,128)} %copy.49), channel_id=1, source_target_pairs={{16,0},{32,16},{48,32},{64,48},{80,64},{96,80},{112,96},{0,112},{1... | collective-permute-start | bytes 1572872 | tf_op jit(solution)/shard_map/while/body/eval_jaxpr/ppermute | solution.py:15
  220.1 23.3 %collective-permute-start = (f32[128,1024]{0,1:T(8,128)}, f32[128,1024]{0,1:T(8,128)}, u32[]{:S(2)}, u32[]{:S(2)}) collective-permute-start(f32[128,1024]{0,1:T(8,128)} %copy.48), channel_id=1, source_target_pairs={{1,0},{2,1},{3,2},{4,3},{5,4},{6,5},{7,6},{8,7},{9,8},{10,9},{11,1... | collective-permute-start | bytes 1572872 | tf_op jit(solution)/shard_map/while/body/eval_jaxpr/ppermute | solution.py:15
  245.4 23.3 %collective-permute-start = (f32[128,1024]{0,1:T(8,128)}, f32[128,1024]{0,1:T(8,128)}, u32[]{:S(2)}, u32[]{:S(2)}) collective-permute-start(f32[128,1024]{0,1:T(8,128)} %copy.48), channel_id=1, source_target_pairs={{1,0},{2,1},{3,2},{4,3},{5,4},{6,5},{7,6},{8,7},{9,8},{10,9},{11,1... | collective-permute-start | bytes 1572872 | tf_op jit(solution)/shard_map/while/body/eval_jaxpr/ppermute | solution.py:15
  250.2 18.5 %collective-permute-start.1 = (f32[2,64,1024]{2,1,0:T(8,128)}, f32[2,64,1024]{2,1,0:T(8,128)}, u32[]{:S(2)}, u32[]{:S(2)}) collective-permute-start(f32[2,64,1024]{2,1,0:T(8,128)} %copy.49), channel_id=1, source_target_pairs={{16,0},{32,16},{48,32},{64,48},{80,64},{96,80},{112,96},{0,112},{1... | collective-permute-start | bytes 1572872 | tf_op jit(solution)/shard_map/while/body/eval_jaxpr/ppermute | solution.py:15
  270.6 23.3 %collective-permute-start = (f32[128,1024]{0,1:T(8,128)}, f32[128,1024]{0,1:T(8,128)}, u32[]{:S(2)}, u32[]{:S(2)}) collective-permute-start(f32[128,1024]{0,1:T(8,128)} %copy.48), channel_id=1, source_target_pairs={{1,0},{2,1},{3,2},{4,3},{5,4},{6,5},{7,6},{8,7},{9,8},{10,9},{11,1... | collective-permute-start | bytes 1572872 | tf_op jit(solution)/shard_map/while/body/eval_jaxpr/ppermute | solution.py:15
  295.8 23.3 %collective-permute-start = (f32[128,1024]{0,1:T(8,128)}, f32[128,1024]{0,1:T(8,128)}, u32[]{:S(2)}, u32[]{:S(2)}) collective-permute-start(f32[128,1024]{0,1:T(8,128)} %copy.48), channel_id=1, source_target_pairs={{1,0},{2,1},{3,2},{4,3},{5,4},{6,5},{7,6},{8,7},{9,8},{10,9},{11,1... | collective-permute-start | bytes 1572872 | tf_op jit(solution)/shard_map/while/body/eval_jaxpr/ppermute | solution.py:15
  300.6 18.5 %collective-permute-start.1 = (f32[2,64,1024]{2,1,0:T(8,128)}, f32[2,64,1024]{2,1,0:T(8,128)}, u32[]{:S(2)}, u32[]{:S(2)}) collective-permute-start(f32[2,64,1024]{2,1,0:T(8,128)} %copy.49), channel_id=1, source_target_pairs={{16,0},{32,16},{48,32},{64,48},{80,64},{96,80},{112,96},{0,112},{1... | collective-permute-start | bytes 1572872 | tf_op jit(solution)/shard_map/while/body/eval_jaxpr/ppermute | solution.py:15
  321.0 23.3 %collective-permute-start = (f32[128,1024]{0,1:T(8,128)}, f32[128,1024]{0,1:T(8,128)}, u32[]{:S(2)}, u32[]{:S(2)}) collective-permute-start(f32[128,1024]{0,1:T(8,128)} %copy.48), channel_id=1, source_target_pairs={{1,0},{2,1},{3,2},{4,3},{5,4},{6,5},{7,6},{8,7},{9,8},{10,9},{11,1... | collective-permute-start | bytes 1572872 | tf_op jit(solution)/shard_map/while/body/eval_jaxpr/ppermute | solution.py:15
  346.3 23.3 %collective-permute-start = (f32[128,1024]{0,1:T(8,128)}, f32[128,1024]{0,1:T(8,128)}, u32[]{:S(2)}, u32[]{:S(2)}) collective-permute-start(f32[128,1024]{0,1:T(8,128)} %copy.48), channel_id=1, source_target_pairs={{1,0},{2,1},{3,2},{4,3},{5,4},{6,5},{7,6},{8,7},{9,8},{10,9},{11,1... | collective-permute-start | bytes 1572872 | tf_op jit(solution)/shard_map/while/body/eval_jaxpr/ppermute | solution.py:15
  351.1 18.5 %collective-permute-start.1 = (f32[2,64,1024]{2,1,0:T(8,128)}, f32[2,64,1024]{2,1,0:T(8,128)}, u32[]{:S(2)}, u32[]{:S(2)}) collective-permute-start(f32[2,64,1024]{2,1,0:T(8,128)} %copy.49), channel_id=1, source_target_pairs={{16,0},{32,16},{48,32},{64,48},{80,64},{96,80},{112,96},{0,112},{1... | collective-permute-start | bytes 1572872 | tf_op jit(solution)/shard_map/while/body/eval_jaxpr/ppermute | solution.py:15
  371.4 23.4 %collective-permute-start = (f32[128,1024]{0,1:T(8,128)}, f32[128,1024]{0,1:T(8,128)}, u32[]{:S(2)}, u32[]{:S(2)}) collective-permute-start(f32[128,1024]{0,1:T(8,128)} %copy.48), channel_id=1, source_target_pairs={{1,0},{2,1},{3,2},{4,3},{5,4},{6,5},{7,6},{8,7},{9,8},{10,9},{11,1... | collective-permute-start | bytes 1572872 | tf_op jit(solution)/shard_map/while/body/eval_jaxpr/ppermute | solution.py:15
  396.7 23.3 %collective-permute-start = (f32[128,1024]{0,1:T(8,128)}, f32[128,1024]{0,1:T(8,128)}, u32[]{:S(2)}, u32[]{:S(2)}) collective-permute-start(f32[128,1024]{0,1:T(8,128)} %copy.48), channel_id=1, source_target_pairs={{1,0},{2,1},{3,2},{4,3},{5,4},{6,5},{7,6},{8,7},{9,8},{10,9},{11,1... | collective-permute-start | bytes 1572872 | tf_op jit(solution)/shard_map/while/body/eval_jaxpr/ppermute | solution.py:15
  401.5 18.5 %collective-permute-start.1 = (f32[2,64,1024]{2,1,0:T(8,128)}, f32[2,64,1024]{2,1,0:T(8,128)}, u32[]{:S(2)}, u32[]{:S(2)}) collective-permute-start(f32[2,64,1024]{2,1,0:T(8,128)} %copy.49), channel_id=1, source_target_pairs={{16,0},{32,16},{48,32},{64,48},{80,64},{96,80},{112,96},{0,112},{1... | collective-permute-start | bytes 1572872 | tf_op jit(solution)/shard_map/while/body/eval_jaxpr/ppermute | solution.py:15
  421.9 23.3 %collective-permute-start = (f32[128,1024]{0,1:T(8,128)}, f32[128,1024]{0,1:T(8,128)}, u32[]{:S(2)}, u32[]{:S(2)}) collective-permute-start(f32[128,1024]{0,1:T(8,128)} %copy.48), channel_id=1, source_target_pairs={{1,0},{2,1},{3,2},{4,3},{5,4},{6,5},{7,6},{8,7},{9,8},{10,9},{11,1... | collective-permute-start | bytes 1572872 | tf_op jit(solution)/shard_map/while/body/eval_jaxpr/ppermute | solution.py:15
  (12 other events, 166.0 us)
where the time goes:
time: 539 us; the launch traced here: 534 us
  local copies, waits for them, and re-layouts  243 us (45%)
  matrix products  112 us (21%)
  blocking collectives  64.8 us (12%)
  starting transfers between devices  56.8 us (11%)
  other arithmetic  28.4 us (5%)
  waiting for transfers between devices  25.4 us (5%)
    dot_general x16, matrix products, step_product(): jnp.einsum('raxz,raczy->rcxy', left_blocks, routed, precision=HIGHEST)  112 us
    psum x1, blocking collectives, shards(): total_trace = lax.psum(jnp.sum(diagonal * traces), ('row', 'col'))  64.8 us
    another operation x16, local copies, waits for them, and re-layouts  61.6 us
    while x30, local copies, waits for them, and re-layouts  56.5 us
    dot_general x16, local copies, waits for them, and re-layouts, step_product(): routed = jnp.einsum('racb,rabxy->racxy', matches, chosen, precision=HIGHEST)  45.4 us
    ppermute x30, starting transfers between devices, shifted(): return lax.ppermute(block, axis, route)  45.3 us
    all_to_all x1, waiting for transfers between devices, shards(): lax.all_to_all(outgoing.reshape(owners, 2 * halves * slot_depth, flat_wid...  25.3 us
    squeeze x16, local copies, waits for them, and re-layouts, pick_right(): return right_now[group_index // row_count]  16 us
  transfers between devices with their start and end apart: 31, of which 1 were waited for; matrix products, arithmetic and copies ran while one was open for 57% of the time, Pallas kernels for 0%

commit v1 on v0

v1 whole, which is shorter than its diff:
```python
import functools

import jax
import jax.numpy as jnp
from jax import lax
from jax.experimental import pallas as pl
from jax.experimental.pallas import tpu as pltpu
from jax.sharding import PartitionSpec as P

BS = 32
AREA = BS * BS
SUB, LANES = 8, 128
R, C = 8, 16
HALF = 64
CAP_L = 12
CAP_R = 16
MESH = pl.DeviceIdType.MESH
F32, I32, BF16 = jnp.float32, jnp.int32, jnp.bfloat16
HIGHEST = lax.Precision.HIGHEST


def iota(shape, axis):
    return lax.broadcasted_iota(I32, shape, axis)


def lookup(table, index):
    return jnp.take_along_axis(table, index, axis=1, mode="promise_in_bounds")


def block_products(left, right, out, accumulate):
    def rows(step, carry):
        base = pl.multiple_of(step * (4 * BS), 4 * BS)
        totals = [[None] * 4 for _ in range(4)]
        for z in range(BS):
            tiles = [right[pl.ds(z * BS + 8 * q, 8), :] for q in range(4)]
            for x in range(4):
                factor = jnp.broadcast_to(left[pl.ds(base + x * BS + z, 1), :], (8, LANES))
                for q in range(4):
                    term = factor * tiles[q]
                    totals[x][q] = term if totals[x][q] is None else totals[x][q] + term
        for x in range(4):
            for q in range(4):
                spot = pl.ds(base + x * BS + 8 * q, 8)
                value = totals[x][q]
                out[spot, :] = out[spot, :] + value if accumulate else value
        return carry

    lax.fori_loop(0, BS // 4, rows, 0)


def to_lanes(stacked, out, keep=None):
    for s in range(SUB):
        piece = jnp.transpose(stacked[:, s, :])
        if keep is not None:
            piece = piece * keep
        out[s * LANES : (s + 1) * LANES, :] = piece


def kernel(
    blocks, cols, slots, keep,
    out, aux, panel_out,
    xv, land, agr, dcol, ctb, ct3, tt, lists_v, lists,
    panel, sorted_a, sorted_b, ta, tb, tc, ot,
    lpack, rpack, lland, rland, onehot, tr_src, tr_land,
    in_sem, ct_sem, self_sem, list_sem, out_sem,
    sr_send, sc_send, sr_recv, sc_recv,
    t1_send, t1_recv, ar_send, ac_send, ar_recv, ac_recv, fw_send, fw_recv,
    xl_send, xr_send, xl_recv, xr_recv, tr_send, tr_recv,
):
    r = lax.axis_index("row")
    c = lax.axis_index("col")
    me = r * C + c
    p, q = c % 2, c // 2
    partner = c + 1 - 2 * p

    def remote(src, dst, send, recv, row, col):
        return pltpu.make_async_remote_copy(
            src_ref=src, dst_ref=dst, send_sem=send, recv_sem=recv,
            device_id=(row, col), device_id_type=MESH,
        )

    def drain(ref, sem):
        pltpu.make_async_copy(ref, ref, sem).wait()

    loads = [
        pltpu.make_async_copy(blocks.at[:, :, pl.ds(LANES * t, LANES)], xv.at[:, :, t, :], in_sem.at[t])
        for t in range(SUB)
    ]
    for copy in loads:
        copy.start()
    tables = []
    for b in range(R):
        piece = cols.at[:, pl.ds(LANES * b, LANES)]
        tables.append(pltpu.make_async_copy(piece, ctb.at[b], ct_sem.at[4 * b]))
        tables.append(pltpu.make_async_copy(piece, ct3.at[:, b, :], ct_sem.at[4 * b + 1]))
        tables.append(pltpu.make_async_copy(piece, tt.at[:, 2 * b, :], ct_sem.at[4 * b + 2]))
        tables.append(pltpu.make_async_copy(piece, tt.at[:, 2 * b + 1, :], ct_sem.at[4 * b + 3]))
    for copy in tables:
        copy.start()

    barrier = pltpu.get_barrier_semaphore()

    def greet(k, carry):
        d = (me + k) % (R * C)
        pl.semaphore_signal(barrier, inc=1, device_id=(d // C, d % C), device_id_type=MESH)
        return carry

    lax.fori_loop(1, R * C, greet, 0)
    for copy in loads:
        copy.wait()
    pl.semaphore_wait(barrier, R * C - 1)

    def row_scatter(k, carry):
        rr = (r + k) % R
        for h in range(2):
            g = 2 * rr + h
            remote(xv.at[g, g], agr.at[(p * 8 + q) * 16 + r * 2 + h], sr_send, sr_recv, rr, c).start()
        return carry

    lax.fori_loop(1, R, row_scatter, 0)

    def col_scatter(k, carry):
        g = (c + k) % C
        remote(xv.at[g, g], dcol.at[r * C + c], sc_send, sc_recv, r, g).start()
        return carry

    lax.fori_loop(1, C, col_scatter, 0)

    def exchange(k, carry):
        d = (me + k * 37) % (R * C)
        rr, cc = d // C, d % C
        remote(xv.at[pl.ds(2 * rr, 2), cc], land.at[pl.ds(2 * me, 2)], t1_send, t1_recv, rr, cc).start()
        return carry

    lax.fori_loop(1, R * C, exchange, 0)
    own = [
        pltpu.make_async_copy(xv.at[2 * r, 2 * r], agr.at[(p * 8 + q) * 16 + r * 2], self_sem.at[0]),
        pltpu.make_async_copy(xv.at[2 * r + 1, 2 * r + 1], agr.at[(p * 8 + q) * 16 + r * 2 + 1], self_sem.at[1]),
        pltpu.make_async_copy(xv.at[c, c], dcol.at[r * C + c], self_sem.at[2]),
        pltpu.make_async_copy(xv.at[pl.ds(2 * r, 2), c], land.at[pl.ds(2 * me, 2)], self_sem.at[3]),
    ]
    for copy in own:
        copy.start()

    for copy in tables:
        copy.wait()
    lane8, lane16 = iota((8, LANES), 1), iota((C, LANES), 1)
    sub8, sub16 = iota((8, LANES), 0), iota((C, LANES), 0)
    ones = jnp.ones((LANES, LANES), BF16)

    def prefix(value, axis):
        place, total, step = iota(value.shape, axis), value, 1
        while step < value.shape[axis]:
            total = total + jnp.where(place >= step, pltpu.roll(total, step, axis), 0)
            step *= 2
        return total - value

    def count_before(flags):
        return prefix(flags.astype(I32), 1)

    def count(flags):
        return jnp.sum(flags.astype(I32), axis=1, keepdims=True)

    def count_fast(flags):
        return jnp.dot(flags.astype(BF16), ones, preferred_element_type=F32).astype(I32)

    own_group = 2 * r + (lane16 // HALF)
    mine = ctb[r]
    target = jnp.broadcast_to(ctb[r, pl.ds(c, 1), :], (C, LANES))
    found = lookup(tt[c], mine % LANES)
    hit = (found == target) & (sub16 != c) & (sub16 != own_group)
    rank = count_before(hit)
    total = jnp.broadcast_to(count(hit), (C, LANES))
    first = prefix(total, 0) + rank
    in_pair = jnp.where(sub16 % 2 == 1, pltpu.roll(total, 1, 0), 0) + rank
    spot_a = jnp.minimum(sub16 * CAP_L + rank, C * CAP_L - 1)
    spot_b = jnp.minimum((sub16 // 2) * CAP_R + in_pair, R * CAP_R - 1)
    spots = spot_a + 256 * spot_b
    rows = iota((LANES, LANES), 0)
    chosen = jnp.zeros((LANES, LANES), I32)
    picks = jnp.zeros((LANES, LANES), I32)
    order = jnp.where(hit, first, -1)
    for m in range(C):
        spread = rows == order[m : m + 1, :]
        chosen = jnp.where(spread, 1, chosen)
        picks = jnp.where(spread, spots[m : m + 1, :], picks)
    onehot[...] = chosen.astype(BF16)
    picks = jnp.broadcast_to(jnp.sum(picks, axis=1, keepdims=True), (LANES, LANES))
    picks = jnp.transpose(picks)[0:8, :]

    owner = slots[pl.ds(r, 1), :] // C
    far_owner = lookup(
        jnp.broadcast_to(slots[pl.ds(q, 1), :] // C, (8, LANES)),
        jnp.broadcast_to(ctb[r, pl.ds(c, 1), :] % LANES, (8, LANES)),
    )
    owner8 = jnp.broadcast_to(owner, (8, LANES))
    half = lane8 // HALF
    o_col, o_row = owner8 % C, owner8 // C
    at_land = 2 * owner8 + half
    at_agr = (((o_col % 2) * 8 + o_col // 2) * 8 + o_row) * 2 + half
    head = jnp.where(sub8 == 0, at_land, jnp.where(sub8 == 1, at_agr, far_owner))
    head = jnp.where(sub8 == 3, picks % 256, jnp.where(sub8 == 4, picks // 256, head))
    lists_v[0:8, :] = head

    left_index = jnp.broadcast_to(ctb[r, pl.ds(c, 1), :] % LANES, (C, LANES))
    left_found = lookup(ctb[q], left_index)
    left_hit = (left_found == mine) & (sub16 != c) & (own_group != c)
    left_rank = count_before(left_hit)
    left_list = jnp.zeros((C, LANES), I32)
    for k in range(CAP_L):
        value = jnp.sum(jnp.where(left_hit & (left_rank == k), lane16, 0), axis=1, keepdims=True)
        left_list = jnp.where(lane16 == k, value, left_list)
    lists_v[8:24, :] = left_list

    right_target = ct3[c]
    right_table = jnp.broadcast_to(ct3[c, pl.ds(r, 1), :], (8, LANES))
    their_group = 2 * sub8 + half
    right_list = jnp.zeros((8, LANES), I32)
    flags, places, ranks = [], [], []
    for h in range(2):
        m = 2 * r + h
        place = ct3[m] % LANES
        right_hit = (lookup(right_table, place) == right_target) & (m != c) & (their_group != m)
        right_rank = count_before(right_hit)
        if h == 1:
            right_rank = right_rank + count(flags[0])
        flags.append(right_hit)
        places.append(place)
        ranks.append(right_rank)
    for k in range(CAP_R):
        value = sum(
            jnp.sum(jnp.where(flags[h] & (ranks[h] == k), places[h], 0), axis=1, keepdims=True)
            for h in range(2)
        )
        right_list = jnp.where(lane8 == k, value, right_list)
    lists_v[24:32, :] = right_list
    to_smem = pltpu.make_async_copy(lists_v, lists, list_sem)
    to_smem.start()

    even = sub16 % 2 == 0

    def survey(step, worst):
        row, col = step // C, step % C
        theirs = ctb[row]
        wanted = jnp.broadcast_to(ct3[col, pl.ds(row, 1), :], (C, LANES))
        seen = lookup(tt[col], theirs % LANES)
        group = 2 * row + (lane16 // HALF)
        used = count_fast((seen == wanted) & (sub16 != col) & (sub16 != group))
        pair = jnp.where(even, used + pltpu.roll(used, C - 1, 0), 0)
        whole = jnp.sum(used, axis=0, keepdims=True)
        over = jnp.maximum(used - CAP_L, pair - CAP_R)
        return jnp.maximum(worst, jnp.maximum(over, whole - LANES))

    worst = lax.fori_loop(0, R * C, survey, jnp.full((C, LANES), -1, I32))
    to_smem.wait()
    for copy in own:
        copy.wait()

    piece = agr.at[pl.ds((p * 8 + q) * 16, 16)]
    column_piece = dcol.at[pl.ds(r * C, C)]
    drain(agr.at[pl.ds(0, 2 * (R - 1))], sr_recv)
    drain(dcol.at[pl.ds(0, C - 1)], sc_recv)

    def row_gather(k, carry):
        cc = (c + 2 * k) % C
        remote(piece, piece, ar_send, ar_recv, r, cc).start()
        return carry

    lax.fori_loop(1, C // 2, row_gather, 0)

    def col_gather(k, carry):
        remote(column_piece, column_piece, ac_send, ac_recv, (r + k) % R, c).start()
        return carry

    lax.fori_loop(1, R, col_gather, 0)

    drain(land.at[pl.ds(0, 2 * (R * C - 1))], t1_recv)

    def collect(i, carry):
        panel[i] = land[jnp.clip(lists[0, i], 0, 2 * R * C - 1)]
        return carry

    lax.fori_loop(0, LANES, collect, 0, unroll=8)

    def pack_left(d, carry):
        for k in range(CAP_L):
            lpack[d * CAP_L + k] = panel[jnp.clip(lists[8 + d, k], 0, LANES - 1)]
        return carry

    lax.fori_loop(0, C, pack_left, 0)

    def send_left(k, carry):
        cc = (c + k) % C
        remote(lpack.at[pl.ds(cc * CAP_L, CAP_L)], lland.at[pl.ds(c * CAP_L, CAP_L)], xl_send, xl_recv, r, cc).start()
        return carry

    lax.fori_loop(1, C, send_left, 0)

    def pack_right(d, carry):
        for k in range(CAP_R):
            rpack[d * CAP_R + k] = panel[jnp.clip(lists[24 + d, k], 0, LANES - 1)]
        return carry

    lax.fori_loop(0, R, pack_right, 0)

    def send_right(k, carry):
        rr = (r + k) % R
        remote(rpack.at[pl.ds(rr * CAP_R, CAP_R)], rland.at[pl.ds(r * CAP_R, CAP_R)], xr_send, xr_recv, rr, c).start()
        return carry

    lax.fori_loop(1, R, send_right, 0)
    keep_left = pltpu.make_async_copy(
        lpack.at[pl.ds(c * CAP_L, CAP_L)], lland.at[pl.ds(c * CAP_L, CAP_L)], self_sem.at[4]
    )
    keep_right = pltpu.make_async_copy(
        rpack.at[pl.ds(r * CAP_R, CAP_R)], rland.at[pl.ds(r * CAP_R, CAP_R)], self_sem.at[5]
    )
    keep_left.start()
    keep_right.start()
    save = pltpu.make_async_copy(panel, panel_out, out_sem)
    save.start()

    drain(agr.at[pl.ds(0, 16 * (C // 2 - 1))], ar_recv)
    forward = remote(agr.at[pl.ds(p * 128, 128)], agr.at[pl.ds(p * 128, 128)], fw_send, fw_recv, r, partner)
    forward.start()

    to_lanes(panel, tb)
    drain(dcol.at[pl.ds(0, C * (R - 1))], ac_recv)

    def collect_column(i, carry):
        sorted_b[i] = dcol[jnp.clip(lists[2, i], 0, R * C - 1)]
        return carry

    lax.fori_loop(0, LANES, collect_column, 0, unroll=8)
    to_lanes(sorted_b, tc)
    block_products(tb, tc, ot, False)
    forward.wait()

    def collect_row(i, carry):
        sorted_a[i] = agr[jnp.clip(lists[1, i], 0, 2 * R * C - 1)]
        return carry

    lax.fori_loop(0, LANES, collect_row, 0, unroll=8)
    lane1 = iota((1, LANES), 1)
    group1 = 2 * r + lane1 // HALF
    to_lanes(sorted_a, ta, (group1 != c).astype(F32))
    block_products(ta, tb, ot, True)

    keep_left.wait()
    keep_right.wait()
    drain(lland.at[pl.ds(0, (C - 1) * CAP_L)], xl_recv)
    drain(rland.at[pl.ds(0, (R - 1) * CAP_R)], xr_recv)

    def collect_pairs(i, carry):
        sorted_a[i] = lland[jnp.clip(lists[3, i], 0, C * CAP_L - 1)]
        sorted_b[i] = rland[jnp.clip(lists[4, i], 0, R * CAP_R - 1)]
        return carry

    lax.fori_loop(0, LANES, collect_pairs, 0, unroll=8)
    to_lanes(sorted_a, ta)
    to_lanes(sorted_b, tc)
    block_products(ta, tc, tb, False)
    spread = onehot[...]
    for s in range(SUB):
        spot = slice(s * LANES, (s + 1) * LANES)
        value = tb[spot, :]
        high = value.astype(BF16)
        rest = value - high.astype(F32)
        middle = rest.astype(BF16)
        low = (rest - middle.astype(F32)).astype(BF16)
        moved = jnp.dot(low, spread, preferred_element_type=F32)
        moved = moved + jnp.dot(middle, spread, preferred_element_type=F32)
        moved = moved + jnp.dot(high, spread, preferred_element_type=F32)
        ot[spot, :] = ot[spot, :] + moved

    diagonal = ot[0:1, :]
    for x in range(1, BS):
        diagonal = diagonal + ot[33 * x : 33 * x + 1, :]
    partial = jnp.sum(jnp.where(group1 == c, diagonal, 0.0), axis=1, keepdims=True)
    tr_src[...] = jnp.broadcast_to(partial, (SUB, LANES))
    source = q == r

    @pl.when(source)
    def _():
        tr_land[c] = jnp.broadcast_to(partial, (SUB, LANES))

        def tell(k, carry):
            d = (me + k) % (R * C)
            remote(tr_src, tr_land.at[c], tr_send, tr_recv, d // C, d % C).start()
            return carry

        lax.fori_loop(1, R * C, tell, 0)

    kept = keep[...].astype(F32)
    for s in range(SUB):
        spot = slice(s * LANES, (s + 1) * LANES)
        out[:, spot] = jnp.transpose(ot[spot, :] * kept)

    @pl.when(source)
    def _():
        drain(tr_land.at[pl.ds(0, C - 1)], tr_recv)
        drain(land.at[pl.ds(0, R * C - 1)], tr_send)

    @pl.when(jnp.logical_not(source))
    def _():
        drain(tr_land, tr_recv)

    trace = tr_land[0]
    for k in range(1, C):
        trace = trace + tr_land[k]
    limit = jnp.max(worst, axis=0, keepdims=True)
    limit = jnp.max(limit, axis=1, keepdims=True)
    aux[...] = jnp.where(sub8 == 0, trace / (R * LANES), jnp.broadcast_to(limit, (8, LANES)).astype(F32))

    save.wait()
    drain(agr.at[pl.ds(0, 2 * (R - 1))], sr_send)
    drain(dcol.at[pl.ds(0, C - 1)], sc_send)
    drain(land.at[pl.ds(0, 2 * (R * C - 1))], t1_send)
    drain(agr.at[pl.ds(0, 16 * (C // 2 - 1))], ar_send)
    drain(dcol.at[pl.ds(0, C * (R - 1))], ac_send)
    drain(lland.at[pl.ds(0, (C - 1) * CAP_L)], xl_send)
    drain(rland.at[pl.ds(0, (R - 1) * CAP_R)], xr_send)


def sparse_product(blocks, cols, slots, keep):
    tile = (SUB, LANES)
    dma = pltpu.SemaphoreType.DMA
    wide = pltpu.VMEM((AREA, LANES), F32)
    batch = pltpu.VMEM((LANES,) + tile, F32)
    vmem = pl.BlockSpec(memory_space=pltpu.VMEM)
    hbm = pl.BlockSpec(memory_space=pl.ANY)
    return pl.pallas_call(
        kernel,
        out_shape=(
            jax.ShapeDtypeStruct((LANES, AREA), F32),
            jax.ShapeDtypeStruct(tile, F32),
            jax.ShapeDtypeStruct((LANES,) + tile, F32),
        ),
        in_specs=[hbm, hbm, vmem, vmem],
        out_specs=(vmem, vmem, hbm),
        scratch_shapes=[
            pltpu.VMEM((C, C) + tile, F32),
            pltpu.VMEM((2 * R * C,) + tile, F32),
            pltpu.VMEM((2 * R * C,) + tile, F32),
            pltpu.VMEM((R * C,) + tile, F32),
            pltpu.VMEM((R, C, LANES), I32),
            pltpu.VMEM((C, R, LANES), I32),
            pltpu.VMEM((C, C, LANES), I32),
            pltpu.VMEM((32, LANES), I32),
            pltpu.SMEM((32, LANES), I32),
            batch, batch, batch,
            wide, wide, wide, wide,
            pltpu.VMEM((C * CAP_L,) + tile, F32),
            pltpu.VMEM((R * CAP_R,) + tile, F32),
            pltpu.VMEM((C * CAP_L,) + tile, F32),
            pltpu.VMEM((R * CAP_R,) + tile, F32),
            pltpu.VMEM((LANES, LANES), BF16),
            pltpu.VMEM(tile, F32),
            pltpu.VMEM((C,) + tile, F32),
            dma((SUB,)), dma((4 * R,)), dma((6,)), dma, dma,
        ] + [dma] * 18,
        compiler_params=pltpu.CompilerParams(collective_id=0, has_side_effects=True),
    )(blocks, cols, slots, keep)


def dense_product(panel, columns, keep):
    r, c = lax.axis_index("row"), lax.axis_index("col")
    mine = lax.dynamic_slice_in_dim(columns, r * LANES, LANES)
    target = lax.dynamic_slice_in_dim(mine, c, 1, 1)[:, 0]
    far_all = lax.dynamic_slice_in_dim(columns, c, 1, 1)[:, 0]
    flat = panel.reshape(LANES, AREA)

    def around(value, axis):
        size = lax.axis_size(axis)
        return lax.ppermute(value, axis, [((i + 1) % size, i) for i in range(size)])

    def gather(step, carry):
        rights, moving = carry
        rights = lax.dynamic_update_slice_in_dim(rights, moving[None], (r + step) % R, 0)
        return rights, around(moving, "row")

    rights, _ = lax.fori_loop(0, R, gather, (jnp.zeros((R, LANES, AREA), F32), flat))
    rights = rights.reshape(R * LANES, AREA)

    def advance(step, carry):
        totals, left = carry
        m = (c + step) % C
        inner = lax.dynamic_slice_in_dim(mine, m, 1, 1)[:, 0]
        match = (far_all[inner] == target).astype(F32)
        right = rights[inner] * match[:, None]
        term = jnp.einsum(
            "nxz,nzy->nxy", left.reshape(LANES, BS, BS), right.reshape(LANES, BS, BS), precision=HIGHEST
        )
        return totals + term, around(left, "col")

    totals, _ = lax.fori_loop(0, C, advance, (jnp.zeros((LANES, BS, BS), F32), flat))
    ids = r * LANES + jnp.arange(LANES, dtype=I32)
    traces = jnp.trace(totals, axis1=1, axis2=2)
    trace = jnp.full((8, LANES), jnp.sum(jnp.where(target == ids, traces, 0.0)))
    for axis in ("row", "col"):
        def add(step, carry):
            total, moving = carry
            moving = around(moving, axis)
            return total + moving, moving
        trace, _ = lax.fori_loop(1, lax.axis_size(axis), add, (trace, trace))
    filtered = totals.reshape(LANES, AREA) * keep.reshape(LANES, 1).astype(F32)
    return filtered, trace[0, 0] / (R * LANES)


def shards(blocks, columns, owner_slot, keep_mask):
    keep = keep_mask.T
    filtered, aux, panel = sparse_product(blocks, columns.T, owner_slot.reshape(R, LANES), keep)
    filtered, trace = lax.cond(
        aux[1, 0] > 0,
        lambda f, t, s: dense_product(s, columns, keep),
        lambda f, t, s: (f, t),
        filtered, aux[0, 0], panel,
    )
    return filtered.reshape(LANES, 1, AREA), trace


def solution(mesh):
    in_specs = (P(("row", "col"), None, None), P(), P(), P("row", "col"))
    out_specs = (P("row", "col", None), P())
    return jax.shard_map(shards, mesh=mesh, in_specs=in_specs, out_specs=out_specs, check_vma=False)
```

time: 539 us -> 88.9 us (0.16)
  local copies, waits for them, and re-layouts: 243 us -> 2.25 us
  matrix products: 112 us -> 0 us
  Pallas kernels: 0 us -> 85.2 us
  blocking collectives: 64.8 us -> 0 us
  starting transfers between devices: 56.8 us -> 0 us
  other arithmetic: 28.4 us -> 0 us
  waiting for transfers between devices: 25.4 us -> 0 us
    dot_general x16 -> x0, matrix products: 112 us -> none  [step_product(): jnp.einsum('raxz,raczy->rcxy', left_blocks, routed, precision=HIGHEST)]
    pallas_call x0 -> x1, Pallas kernels: none -> 85.2 us  [sparse_product(): pl.pallas_call(kernel, out_shape=(jax.ShapeDtypeStruct((LANES, AREA), F32...]
    another operation x22 -> x1, local copies, waits for them, and re-layouts: 67.1 us -> 0.19 us
    psum x1 -> x0, blocking collectives: 64.8 us -> none  [shards(): total_trace = lax.psum(jnp.sum(diagonal * traces), ('row', 'col'))]
    while x30 -> x0, local copies, waits for them, and re-layouts: 56.5 us -> none
    dot_general x16 -> x0, local copies, waits for them, and re-layouts: 45.4 us -> none  [step_product(): routed = jnp.einsum('racb,rabxy->racxy', matches, chosen, precision=HIGHEST)]
    ppermute x30 -> x0, starting transfers between devices: 45.3 us -> none  [shifted(): return lax.ppermute(block, axis, route)]
    gather x54 -> x0, local copies, waits for them, and re-layouts: 40.7 us -> none  [the longest x32 15.8 us: step_product(): right_panel[local_rows].reshape(panel_rows, per_group, per_group, BS, BS)]
  transfers between devices with their start and end apart: 31 -> 0, of which waited for: 1 -> 0; matrix products, arithmetic and copies ran while one was open for 57% -> 0% of each run, Pallas kernels for 0% -> 0%
where the time goes in v1:
time: 88.9 us; the launch traced here: 88.8 us
  Pallas kernels  85.2 us (96%)
  local copies, waits for them, and re-layouts  2.25 us (3%)
  between operations  1.29 us (1%)
    pallas_call x1, Pallas kernels, sparse_product(): pl.pallas_call(kernel, out_shape=(jax.ShapeDtypeStruct((LANES, AREA), F32...  85.2 us

profile of v1, /device:TPU:1, one launch (start us, length us, event | category | flops | bytes accessed | tf_op | source)
XLA Modules:
  0.0 88.8 jit_solution(2901057632028070944)
XLA Ops:
  0.6 85.2 %shard_map.59 = (f32[128,1024]{1,0:T(8,128)S(1)}, f32[8,128]{1,0:T(8,128)S(1)}, f32[128,8,128]{2,1,0:T(8,128)S(1)}) custom-call(f32[16,16,1024]{2,1,0:T(8,128)} %blocks.1, s32[16,1024]{1,0:T(8,128)} %bitcast.47, s32[8,128]{1,0:T(8,128)} %bitcast.48, s32[1,128]{1,0:T(1,128)} %bitcast.49), custom_call_target="tpu_custom_call" | custom-call | tf_op jit(solution)/shard_map/pallas_call | solution.py:432
  85.8 0.5 slice.10
  87.0 1.8 %conditional.1 = (f32[]{:T(128)}, f32[128,1,1024]{2,1,0:T(1,128)}) conditional(s32[]{:T(128)} %bitcast.13, (f32[8,128]{1,0:T(8,128)S(1)}, f32[128,1024]{1,0:T(8,128)S(1)}) %tuple.70, (s32[1024,16]{0,1:T(8,128)}, f32[128,8,128]{2,1,0:T(8,128)S(1)}, s32[128,1]{0,1:T(1,128)}) %tuple.71), branch_computations={%region_0.0_spmd, %region_1.12_spmd} | conditional | flops 51123376 | bytes 26870564 | solution.py:513
  87.0 0.2 copy.13
  87.2 1.0 %copy.16 = f32[128,1,1024]{2,1,0:T(1,128)} copy(f32[128,1,1024]{0,2,1:T(8,128)S(1)} %bitcast.46) | data formatting | bytes 1048576 | tf_op jit(solution)/shard_map/cond
  88.2 0.5 slice.7

commit v2 on v1

--- a/solution.py
+++ b/solution.py
@@ -58,9 +58,9 @@
 
 def kernel(
     blocks, cols, slots, keep,
-    out, aux, panel_out,
+    out, mean_out, over_out, panel_out,
     xv, land, agr, dcol, ctb, ct3, tt, lists_v, lists,
-    panel, sorted_a, sorted_b, ta, tb, tc, ot,
+    panel, sorted_a, sorted_b, ta, tb, tc, ot, tr_all,
     lpack, rpack, lland, rland, onehot, tr_src, tr_land,
     in_sem, ct_sem, self_sem, list_sem, out_sem,
     sr_send, sc_send, sr_recv, sc_recv,
@@ -81,6 +81,15 @@
 
     def drain(ref, sem):
         pltpu.make_async_copy(ref, ref, sem).wait()
+
+    barrier = pltpu.get_barrier_semaphore()
+
+    def greet(k, carry):
+        d = (me + k) % (R * C)
+        pl.semaphore_signal(barrier, inc=1, device_id=(d // C, d % C), device_id_type=MESH)
+        return carry
+
+    lax.fori_loop(1, R * C, greet, 0)
 
     loads = [
         pltpu.make_async_copy(blocks.at[:, :, pl.ds(LANES * t, LANES)], xv.at[:, :, t, :], in_sem.at[t])
@@ -98,56 +107,10 @@
     for copy in tables:
         copy.start()
 
-    barrier = pltpu.get_barrier_semaphore()
-
-    def greet(k, carry):
-        d = (me + k) % (R * C)
-        pl.semaphore_signal(barrier, inc=1, device_id=(d // C, d % C), device_id_type=MESH)
-        return carry
-
-    lax.fori_loop(1, R * C, greet, 0)
-    for copy in loads:
-        copy.wait()
-    pl.semaphore_wait(barrier, R * C - 1)
-
-    def row_scatter(k, carry):
-        rr = (r + k) % R
-        for h in range(2):
-            g = 2 * rr + h
-            remote(xv.at[g, g], agr.at[(p * 8 + q) * 16 + r * 2 + h], sr_send, sr_recv, rr, c).start()
-        return carry
-
-    lax.fori_loop(1, R, row_scatter, 0)
-
-    def col_scatter(k, carry):
-        g = (c + k) % C
-        remote(xv.at[g, g], dcol.at[r * C + c], sc_send, sc_recv, r, g).start()
-        return carry
-
-    lax.fori_loop(1, C, col_scatter, 0)
-
-    def exchange(k, carry):
-        d = (me + k * 37) % (R * C)
-        rr, cc = d // C, d % C
-        remote(xv.at[pl.ds(2 * rr, 2), cc], land.at[pl.ds(2 * me, 2)], t1_send, t1_recv, rr, cc).start()
-        return carry
-
-    lax.fori_loop(1, R * C, exchange, 0)
-    own = [
-        pltpu.make_async_copy(xv.at[2 * r, 2 * r], agr.at[(p * 8 + q) * 16 + r * 2], self_sem.at[0]),
-        pltpu.make_async_copy(xv.at[2 * r + 1, 2 * r + 1], agr.at[(p * 8 + q) * 16 + r * 2 + 1], self_sem.at[1]),
-        pltpu.make_async_copy(xv.at[c, c], dcol.at[r * C + c], self_sem.at[2]),
-        pltpu.make_async_copy(xv.at[pl.ds(2 * r, 2), c], land.at[pl.ds(2 * me, 2)], self_sem.at[3]),
-    ]
-    for copy in own:
-        copy.start()
-
     for copy in tables:
         copy.wait()
     lane8, lane16 = iota((8, LANES), 1), iota((C, LANES), 1)
     sub8, sub16 = iota((8, LANES), 0), iota((C, LANES), 0)
-    ones = jnp.ones((LANES, LANES), BF16)
-
     def prefix(value, axis):
         place, total, step = iota(value.shape, axis), value, 1
         while step < value.shape[axis]:
@@ -160,9 +123,6 @@
 
     def count(flags):
         return jnp.sum(flags.astype(I32), axis=1, keepdims=True)
-
-    def count_fast(flags):
-        return jnp.dot(flags.astype(BF16), ones, preferred_element_type=F32).astype(I32)
 
     own_group = 2 * r + (lane16 // HALF)
     mine = ctb[r]
@@ -197,7 +157,7 @@
     half = lane8 // HALF
     o_col, o_row = owner8 % C, owner8 // C
     at_land = 2 * owner8 + half
-    at_agr = (((o_col % 2) * 8 + o_col // 2) * 8 + o_row) * 2 + half
+    at_agr = (((o_col % 2) * 4 + (o_col // 2) % 4) * 2 + o_col // 8) * 16 + o_row * 2 + half
     head = jnp.where(sub8 == 0, at_land, jnp.where(sub8 == 1, at_agr, far_owner))
     head = jnp.where(sub8 == 3, picks % 256, jnp.where(sub8 == 4, picks // 256, head))
     lists_v[0:8, :] = head
@@ -237,43 +197,75 @@
     to_smem = pltpu.make_async_copy(lists_v, lists, list_sem)
     to_smem.start()
 
+    for copy in loads:
+        copy.wait()
+    pl.semaphore_wait(barrier, R * C - 1)
+
+    row_spot = ((p * 4 + q % 4) * 2 + c // 8) * 16 + r * 2
+    col_spot = r * C + c
+
+    def row_scatter(k, carry):
+        rr, cc = (r + k % R) % R, (c + 8 * (k // R)) % C
+        for h in range(2):
+            g = 2 * rr + h
+            remote(xv.at[g, g], agr.at[row_spot + h], sr_send, sr_recv, rr, cc).start()
+        return carry
+
+    lax.fori_loop(1, 2 * R, row_scatter, 0)
+
+    def col_scatter(k, carry):
+        g, rr = (c + k % C) % C, r + (k // C) * (1 - 2 * (r % 2))
+        remote(xv.at[g, g], dcol.at[col_spot], sc_send, sc_recv, rr, g).start()
+        return carry
+
+    lax.fori_loop(1, 2 * C, col_scatter, 0)
+
+    def exchange(k, carry):
+        d = (me + k * 37) % (R * C)
+        rr, cc = d // C, d % C
+        remote(xv.at[pl.ds(2 * rr, 2), cc], land.at[pl.ds(2 * me, 2)], t1_send, t1_recv, rr, cc).start()
+        return carry
+
+    lax.fori_loop(1, R * C, exchange, 0)
+    own = [
+        pltpu.make_async_copy(xv.at[2 * r, 2 * r], agr.at[row_spot], self_sem.at[0]),
+        pltpu.make_async_copy(xv.at[2 * r + 1, 2 * r + 1], agr.at[row_spot + 1], self_sem.at[1]),
+        pltpu.make_async_copy(xv.at[c, c], dcol.at[r * C + c], self_sem.at[2]),
+        pltpu.make_async_copy(xv.at[pl.ds(2 * r, 2), c], land.at[pl.ds(2 * me, 2)], self_sem.at[3]),
+    ]
+    for copy in own:
+        copy.start()
+
+    for copy in own:
+        copy.wait()
+    piece = agr.at[pl.ds((p * 4 + q % 4) * 32, 32)]
+    column_piece = dcol.at[pl.ds((r // 2) * 32, 32)]
+    drain(agr.at[pl.ds(0, 30)], sr_recv)
+    drain(dcol.at[pl.ds(0, 31)], sc_recv)
+
+    def row_gather(k, carry):
+        cc = (c // 8) * 8 + (c % 8 + 2 * k) % 8
+        remote(piece, piece, ar_send, ar_recv, r, cc).start()
+        return carry
+
+    lax.fori_loop(1, 4, row_gather, 0)
+
+    def col_gather(k, carry):
+        remote(column_piece, column_piece, ac_send, ac_recv, (r + 2 * k) % R, c).start()
+        return carry
+
+    lax.fori_loop(1, 4, col_gather, 0)
+
     even = sub16 % 2 == 0
-
-    def survey(step, worst):
-        row, col = step // C, step % C
-        theirs = ctb[row]
-        wanted = jnp.broadcast_to(ct3[col, pl.ds(row, 1), :], (C, LANES))
-        seen = lookup(tt[col], theirs % LANES)
-        group = 2 * row + (lane16 // HALF)
-        used = count_fast((seen == wanted) & (sub16 != col) & (sub16 != group))
+    worst = jnp.full((C, LANES), -1, I32)
+    for col in range(C):
+        wanted = jnp.broadcast_to(ctb[r, col : col + 1, :], (C, LANES))
+        seen = lookup(tt[col], mine % LANES)
+        used = jnp.broadcast_to(count((seen == wanted) & (sub16 != col) & (sub16 != own_group)), (C, LANES))
         pair = jnp.where(even, used + pltpu.roll(used, C - 1, 0), 0)
         whole = jnp.sum(used, axis=0, keepdims=True)
-        over = jnp.maximum(used - CAP_L, pair - CAP_R)
-        return jnp.maximum(worst, jnp.maximum(over, whole - LANES))
-
-    worst = lax.fori_loop(0, R * C, survey, jnp.full((C, LANES), -1, I32))
+        worst = jnp.maximum(worst, jnp.maximum(jnp.maximum(used - CAP_L, pair - CAP_R), whole - LANES))
     to_smem.wait()
-    for copy in own:
-        copy.wait()
-
-    piece = agr.at[pl.ds((p * 8 + q) * 16, 16)]
-    column_piece = dcol.at[pl.ds(r * C, C)]
-    drain(agr.at[pl.ds(0, 2 * (R - 1))], sr_recv)
-    drain(dcol.at[pl.ds(0, C - 1)], sc_recv)
-
-    def row_gather(k, carry):
-        cc = (c + 2 * k) % C
-        remote(piece, piece, ar_send, ar_recv, r, cc).start()
-        return carry
-
-    lax.fori_loop(1, C // 2, row_gather, 0)
-
-    def col_gather(k, carry):
-        remote(column_piece, column_piece, ac_send, ac_recv, (r + k) % R, c).start()
-        return carry
-
-    lax.fori_loop(1, R, col_gather, 0)
-
     drain(land.at[pl.ds(0, 2 * (R * C - 1))], t1_recv)
 
     def collect(i, carry):
@@ -289,12 +281,19 @@
 
     lax.fori_loop(0, C, pack_left, 0)
 
-    def send_left(k, carry):
+    def send_left(cc):
+        src, dst = lpack.at[pl.ds(cc * CAP_L, CAP_L)], lland.at[pl.ds(c * CAP_L, CAP_L)]
+        remote(src, dst, xl_send, xl_recv, r, cc).start()
+
+    for h in range(2):
+        pl.when(c != 2 * r + h)(functools.partial(send_left, 2 * r + h))
+
+    def send_left_rest(k, carry):
         cc = (c + k) % C
-        remote(lpack.at[pl.ds(cc * CAP_L, CAP_L)], lland.at[pl.ds(c * CAP_L, CAP_L)], xl_send, xl_recv, r, cc).start()
-        return carry
-
-    lax.fori_loop(1, C, send_left, 0)
+        pl.when(cc // 2 != r)(functools.partial(send_left, cc))
+        return carry
+
+    lax.fori_loop(1, C, send_left_rest, 0)
 
     def pack_right(d, carry):
         for k in range(CAP_R):
@@ -303,12 +302,19 @@
 
     lax.fori_loop(0, R, pack_right, 0)
 
-    def send_right(k, carry):
+    def send_right(rr):
+        src, dst = rpack.at[pl.ds(rr * CAP_R, CAP_R)], rland.at[pl.ds(r * CAP_R, CAP_R)]
+        remote(src, dst, xr_send, xr_recv, rr, c).start()
+
+    source = q == r
+    pl.when(jnp.logical_not(source))(functools.partial(send_right, q))
+
+    def send_right_rest(k, carry):
         rr = (r + k) % R
-        remote(rpack.at[pl.ds(rr * CAP_R, CAP_R)], rland.at[pl.ds(r * CAP_R, CAP_R)], xr_send, xr_recv, rr, c).start()
-        return carry
-
-    lax.fori_loop(1, R, send_right, 0)
+        pl.when(rr != q)(functools.partial(send_right, rr))
+        return carry
+
+    lax.fori_loop(1, R, send_right_rest, 0)
     keep_left = pltpu.make_async_copy(
         lpack.at[pl.ds(c * CAP_L, CAP_L)], lland.at[pl.ds(c * CAP_L, CAP_L)], self_sem.at[4]
     )
@@ -320,12 +326,12 @@
     save = pltpu.make_async_copy(panel, panel_out, out_sem)
     save.start()
 
-    drain(agr.at[pl.ds(0, 16 * (C // 2 - 1))], ar_recv)
+    drain(agr.at[pl.ds(0, 96)], ar_recv)
     forward = remote(agr.at[pl.ds(p * 128, 128)], agr.at[pl.ds(p * 128, 128)], fw_send, fw_recv, r, partner)
     forward.start()
 
     to_lanes(panel, tb)
-    drain(dcol.at[pl.ds(0, C * (R - 1))], ac_recv)
+    drain(dcol.at[pl.ds(0, 96)], ac_recv)
 
     def collect_column(i, carry):
         sorted_b[i] = dcol[jnp.clip(lists[2, i], 0, R * C - 1)]
@@ -359,6 +365,33 @@
     lax.fori_loop(0, LANES, collect_pairs, 0, unroll=8)
     to_lanes(sorted_a, ta)
     to_lanes(sorted_b, tc)
+
+    @pl.when(source)
+    def _():
+        diagonal = ot[0:1, :]
+        for x in range(1, BS):
+            diagonal = diagonal + ot[33 * x : 33 * x + 1, :]
+        totals = jnp.zeros((BS, LANES), F32)
+        for x in range(BS):
+            totals = totals + ta[BS * x : BS * (x + 1), :] * tc[pl.ds(x, BS, stride=BS), :]
+        pairs = jnp.sum(totals, axis=0, keepdims=True)
+        inside = jnp.broadcast_to((group1 == c).astype(BF16), (8, LANES))
+        weight = lax.dot_general(inside, onehot[...], (((1,), (1,)), ((), ())), preferred_element_type=F32)
+        partial = jnp.sum(
+            jnp.where(group1 == c, diagonal, 0.0) + pairs * weight[0:1, :], axis=1, keepdims=True
+        )
+        most = jnp.max(jnp.max(worst, axis=0, keepdims=True), axis=1, keepdims=True).astype(F32)
+        told = jnp.where(lane1 < HALF, jnp.broadcast_to(partial, (1, LANES)), jnp.broadcast_to(most, (1, LANES)))
+        tr_src[...] = told
+        tr_land[c] = told
+
+        def tell(k, carry):
+            d = (me + k) % (R * C)
+            remote(tr_src, tr_land.at[c], tr_send, tr_recv, d // C, d % C).start()
+            return carry
+
+        lax.fori_loop(1, R * C, tell, 0)
+
     block_products(ta, tc, tb, False)
     spread = onehot[...]
     for s in range(SUB):
@@ -373,51 +406,33 @@
         moved = moved + jnp.dot(high, spread, preferred_element_type=F32)
         ot[spot, :] = ot[spot, :] + moved
 
-    diagonal = ot[0:1, :]
-    for x in range(1, BS):
-        diagonal = diagonal + ot[33 * x : 33 * x + 1, :]
-    partial = jnp.sum(jnp.where(group1 == c, diagonal, 0.0), axis=1, keepdims=True)
-    tr_src[...] = jnp.broadcast_to(partial, (SUB, LANES))
-    source = q == r
-
-    @pl.when(source)
-    def _():
-        tr_land[c] = jnp.broadcast_to(partial, (SUB, LANES))
-
-        def tell(k, carry):
-            d = (me + k) % (R * C)
-            remote(tr_src, tr_land.at[c], tr_send, tr_recv, d // C, d % C).start()
-            return carry
-
-        lax.fori_loop(1, R * C, tell, 0)
-
     kept = keep[...].astype(F32)
     for s in range(SUB):
         spot = slice(s * LANES, (s + 1) * LANES)
-        out[:, spot] = jnp.transpose(ot[spot, :] * kept)
+        out[:, s, :] = jnp.transpose(ot[spot, :] * kept)
 
     @pl.when(source)
     def _():
         drain(tr_land.at[pl.ds(0, C - 1)], tr_recv)
-        drain(land.at[pl.ds(0, R * C - 1)], tr_send)
+        drain(tr_all, tr_send)
 
     @pl.when(jnp.logical_not(source))
     def _():
         drain(tr_land, tr_recv)
 
-    trace = tr_land[0]
+    trace, most = tr_land[0], tr_land[0]
     for k in range(1, C):
         trace = trace + tr_land[k]
-    limit = jnp.max(worst, axis=0, keepdims=True)
-    limit = jnp.max(limit, axis=1, keepdims=True)
-    aux[...] = jnp.where(sub8 == 0, trace / (R * LANES), jnp.broadcast_to(limit, (8, LANES)).astype(F32))
+        most = jnp.maximum(most, tr_land[k])
+    mean_out[...] = trace[:, 0:1] / (R * LANES)
+    over_out[...] = most[:, HALF : HALF + 1]
 
     save.wait()
-    drain(agr.at[pl.ds(0, 2 * (R - 1))], sr_send)
-    drain(dcol.at[pl.ds(0, C - 1)], sc_send)
+    drain(agr.at[pl.ds(0, 30)], sr_send)
+    drain(dcol.at[pl.ds(0, 31)], sc_send)
     drain(land.at[pl.ds(0, 2 * (R * C - 1))], t1_send)
-    drain(agr.at[pl.ds(0, 16 * (C // 2 - 1))], ar_send)
-    drain(dcol.at[pl.ds(0, C * (R - 1))], ac_send)
+    drain(agr.at[pl.ds(0, 96)], ar_send)
+    drain(dcol.at[pl.ds(0, 96)], ac_send)
     drain(lland.at[pl.ds(0, (C - 1) * CAP_L)], xl_send)
     drain(rland.at[pl.ds(0, (R - 1) * CAP_R)], xr_send)
 
@@ -432,12 +447,13 @@
     return pl.pallas_call(
         kernel,
         out_shape=(
-            jax.ShapeDtypeStruct((LANES, AREA), F32),
-            jax.ShapeDtypeStruct(tile, F32),
+            jax.ShapeDtypeStruct((LANES,) + tile, F32),
+            jax.ShapeDtypeStruct((1, 1), F32),
+            jax.ShapeDtypeStruct((1, 1), F32),
             jax.ShapeDtypeStruct((LANES,) + tile, F32),
         ),
         in_specs=[hbm, hbm, vmem, vmem],
-        out_specs=(vmem, vmem, hbm),
+        out_specs=(vmem, vmem, vmem, hbm),
         scratch_shapes=[
             pltpu.VMEM((C, C) + tile, F32),
             pltpu.VMEM((2 * R * C,) + tile, F32),
@@ -450,13 +466,14 @@
             pltpu.SMEM((32, LANES), I32),
             batch, batch, batch,
             wide, wide, wide, wide,
+            pltpu.VMEM((R * C - 1, 1, LANES), F32),
             pltpu.VMEM((C * CAP_L,) + tile, F32),
             pltpu.VMEM((R * CAP_R,) + tile, F32),
             pltpu.VMEM((C * CAP_L,) + tile, F32),
             pltpu.VMEM((R * CAP_R,) + tile, F32),
             pltpu.VMEM((LANES, LANES), BF16),
-            pltpu.VMEM(tile, F32),
-            pltpu.VMEM((C,) + tile, F32),
+            pltpu.VMEM((1, LANES), F32),
+            pltpu.VMEM((C, 1, LANES), F32),
             dma((SUB,)), dma((4 * R,)), dma((6,)), dma, dma,
         ] + [dma] * 18,
         compiler_params=pltpu.CompilerParams(collective_id=0, has_side_effects=True),
@@ -504,19 +521,19 @@
             return total + moving, moving
         trace, _ = lax.fori_loop(1, lax.axis_size(axis), add, (trace, trace))
     filtered = totals.reshape(LANES, AREA) * keep.reshape(LANES, 1).astype(F32)
-    return filtered, trace[0, 0] / (R * LANES)
+    return filtered.reshape(LANES, SUB, LANES), trace[0, 0] / (R * LANES)
 
 
 def shards(blocks, columns, owner_slot, keep_mask):
     keep = keep_mask.T
-    filtered, aux, panel = sparse_product(blocks, columns.T, owner_slot.reshape(R, LANES), keep)
-    filtered, trace = lax.cond(
-        aux[1, 0] > 0,
+    filtered, mean, over, panel = sparse_product(blocks, columns.T, owner_slot.reshape(R, LANES), keep)
+    filtered, mean = lax.cond(
+        over.reshape(()) > 0,
         lambda f, t, s: dense_product(s, columns, keep),
         lambda f, t, s: (f, t),
-        filtered, aux[0, 0], panel,
+        filtered, mean.reshape(()), panel,
     )
-    return filtered.reshape(LANES, 1, AREA), trace
+    return filtered.reshape(LANES, 1, AREA), mean
 
 
 def solution(mesh):

time: 88.9 us -> 59.7 us (0.67)
  Pallas kernels: 85.2 us -> 55.2 us
  between operations: 1.29 us -> 3.01 us
  local copies, waits for them, and re-layouts: 2.25 us -> 1.27 us
    pallas_call x1, Pallas kernels: 85.2 us -> 55.2 us  [sparse_product(): pl.pallas_call(kernel, out_shape=(jax.ShapeDtypeStruct((LANES,) + tile, F...]
    slice x2 -> x0, local copies, waits for them, and re-layouts: 1.02 us -> none  [the longest x1 0.51 us: shards(): aux[1, 0] > 0]
where the time goes in v2:
time: 59.7 us; the launch traced here: 59.5 us
  Pallas kernels  55.2 us (92%)
  between operations  3.01 us (5%)
  local copies, waits for them, and re-layouts  1.27 us (2%)
    pallas_call x1, Pallas kernels, sparse_product(): pl.pallas_call(kernel, out_shape=(jax.ShapeDtypeStruct((LANES,) + tile, F...  55.2 us

profile of v2, /device:TPU:1, one launch (start us, length us, event | category | flops | bytes accessed | tf_op | source)
XLA Modules:
  0.0 59.5 jit_solution(5734386244682265803)
XLA Ops:
  0.6 55.2 %shard_map.59 = (f32[128,8,128]{2,1,0:T(8,128)S(1)}, f32[1,1]{1,0:T(1,128)}, f32[1,1]{1,0:T(1,128)}, f32[128,8,128]{2,1,0:T(8,128)S(1)}) custom-call(f32[16,16,1024]{2,1,0:T(8,128)} %blocks.1, s32[16,1024]{1,0:T(8,128)} %bitcast.46, s32[8,128]{1,0:T(8,128)} %bitcast.47, s32[1,128]{1,0:T(1,128)} %bitcast.48), custom_call_target="tpu_custom_call" | custom-call | tf_op jit(solution)/shard_map/pallas_call | solution.py:447
  56.5 1.3 %conditional.1 = (f32[1,1]{1,0:T(1,128)}, f32[128,1,1024]{2,1,0:T(1,128)}) conditional(s32[]{:T(128)} %bitcast.11, (f32[1,1]{1,0:T(1,128)}, f32[128,8,128]{2,1,0:T(8,128)S(1)}) %tuple.70, (s32[1024,16]{0,1:T(8,128)}, f32[128,8,128]{2,1,0:T(8,128)S(1)}, s32[128,1]{0,1:T(1,128)}) %tuple.71), branch_computations={%region_0.0_spmd, %region_1.12_spmd} | conditional | flops 51123376 | bytes 26870564 | solution.py:530
  56.6 0.2 copy.13
  56.8 1.0 %copy.16 = f32[128,1,1024]{2,1,0:T(1,128)} copy(f32[128,1,1024]{0,2,1:T(8,128)S(1)} %bitcast.45) | data formatting | bytes 1048576 | tf_op jit(solution)/shard_map/cond

commit v3 on v2

--- a/solution.py
+++ b/solution.py
@@ -12,7 +12,7 @@
 SUB, LANES = 8, 128
 R, C = 8, 16
 HALF = 64
-CAP_L = 12
+CAP_L = 16
 CAP_R = 16
 MESH = pl.DeviceIdType.MESH
 F32, I32, BF16 = jnp.float32, jnp.int32, jnp.bfloat16
@@ -60,12 +60,12 @@
     blocks, cols, slots, keep,
     out, mean_out, over_out, panel_out,
     xv, land, agr, dcol, ctb, ct3, tt, lists_v, lists,
-    panel, sorted_a, sorted_b, ta, tb, tc, ot, tr_all,
-    lpack, rpack, lland, rland, onehot, tr_src, tr_land,
+    panel, sorted_a, sorted_b, ta, tb, tc, ot,
+    lpack, rpack, lland, rland, onehot, tr_row, tr_all,
     in_sem, ct_sem, self_sem, list_sem, out_sem,
     sr_send, sc_send, sr_recv, sc_recv,
     t1_send, t1_recv, ar_send, ac_send, ar_recv, ac_recv, fw_send, fw_recv,
-    xl_send, xr_send, xl_recv, xr_recv, tr_send, tr_recv,
+    xl_send, xr_send, xl_recv, xr_recv, yl_send, yl_recv, tr_send, tr_recv, tc_send, tc_recv,
 ):
     r = lax.axis_index("row")
     c = lax.axis_index("col")
@@ -133,7 +133,11 @@
     total = jnp.broadcast_to(count(hit), (C, LANES))
     first = prefix(total, 0) + rank
     in_pair = jnp.where(sub16 % 2 == 1, pltpu.roll(total, 1, 0), 0) + rank
-    spot_a = jnp.minimum(sub16 * CAP_L + rank, C * CAP_L - 1)
+    ahead = c - p
+    ahead_target = jnp.broadcast_to(ctb[r, pl.ds(ahead, 1), :], (C, LANES))
+    ahead_hit = (lookup(tt[ahead], mine % LANES) == ahead_target) & (sub16 != ahead) & (sub16 != own_group)
+    in_chip = rank + p * count(ahead_hit)
+    spot_a = jnp.minimum(((sub16 % 2) * R + sub16 // 2) * CAP_L + in_chip, C * CAP_L - 1)
     spot_b = jnp.minimum((sub16 // 2) * CAP_R + in_pair, R * CAP_R - 1)
     spots = spot_a + 256 * spot_b
     rows = iota((LANES, LANES), 0)
@@ -166,10 +170,14 @@
     left_found = lookup(ctb[q], left_index)
     left_hit = (left_found == mine) & (sub16 != c) & (own_group != c)
     left_rank = count_before(left_hit)
+    left_total = jnp.broadcast_to(count(left_hit), (C, LANES))
+    left_rank = left_rank + jnp.where(sub16 % 2 == 1, pltpu.roll(left_total, 1, 0), 0)
+    at_land16 = jnp.broadcast_to(at_land[0:1, :], (C, LANES))
     left_list = jnp.zeros((C, LANES), I32)
     for k in range(CAP_L):
-        value = jnp.sum(jnp.where(left_hit & (left_rank == k), lane16, 0), axis=1, keepdims=True)
+        value = jnp.sum(jnp.where(left_hit & (left_rank == k), at_land16, 0), axis=1, keepdims=True)
         left_list = jnp.where(lane16 == k, value, left_list)
+    left_list = left_list + pltpu.roll(left_list, C - 1, 0)
     lists_v[8:24, :] = left_list
 
     right_target = ct3[c]
@@ -185,7 +193,7 @@
         if h == 1:
             right_rank = right_rank + count(flags[0])
         flags.append(right_hit)
-        places.append(place)
+        places.append(lookup(at_land, place))
         ranks.append(right_rank)
     for k in range(CAP_R):
         value = sum(
@@ -258,55 +266,55 @@
 
     even = sub16 % 2 == 0
     worst = jnp.full((C, LANES), -1, I32)
+    before = jnp.zeros((C, LANES), I32)
     for col in range(C):
         wanted = jnp.broadcast_to(ctb[r, col : col + 1, :], (C, LANES))
         seen = lookup(tt[col], mine % LANES)
         used = jnp.broadcast_to(count((seen == wanted) & (sub16 != col) & (sub16 != own_group)), (C, LANES))
         pair = jnp.where(even, used + pltpu.roll(used, C - 1, 0), 0)
         whole = jnp.sum(used, axis=0, keepdims=True)
-        worst = jnp.maximum(worst, jnp.maximum(jnp.maximum(used - CAP_L, pair - CAP_R), whole - LANES))
+        both = used + before if col % 2 else used
+        before = used
+        worst = jnp.maximum(worst, jnp.maximum(jnp.maximum(both - CAP_L, pair - CAP_R), whole - LANES))
     to_smem.wait()
     drain(land.at[pl.ds(0, 2 * (R * C - 1))], t1_recv)
 
-    def collect(i, carry):
-        panel[i] = land[jnp.clip(lists[0, i], 0, 2 * R * C - 1)]
-        return carry
-
-    lax.fori_loop(0, LANES, collect, 0, unroll=8)
-
     def pack_left(d, carry):
         for k in range(CAP_L):
-            lpack[d * CAP_L + k] = panel[jnp.clip(lists[8 + d, k], 0, LANES - 1)]
-        return carry
-
-    lax.fori_loop(0, C, pack_left, 0)
-
-    def send_left(cc):
-        src, dst = lpack.at[pl.ds(cc * CAP_L, CAP_L)], lland.at[pl.ds(c * CAP_L, CAP_L)]
-        remote(src, dst, xl_send, xl_recv, r, cc).start()
-
-    for h in range(2):
-        pl.when(c != 2 * r + h)(functools.partial(send_left, 2 * r + h))
+            lpack[d * CAP_L + k] = land[jnp.clip(lists[8 + 2 * d, k], 0, 2 * R * C - 1)]
+        return carry
+
+    lax.fori_loop(0, R, pack_left, 0)
+    left_spot = pl.ds((p * R + q) * CAP_L, CAP_L)
+
+    def send_left(chip):
+        src = lpack.at[pl.ds(chip * CAP_L, CAP_L)]
+        remote(src, lland.at[left_spot], xl_send, xl_recv, r, 2 * chip + p).start()
+
+    source = q == r
+    pl.when(jnp.logical_not(source))(functools.partial(send_left, r))
 
     def send_left_rest(k, carry):
-        cc = (c + k) % C
-        pl.when(cc // 2 != r)(functools.partial(send_left, cc))
-        return carry
-
-    lax.fori_loop(1, C, send_left_rest, 0)
+        chip = (q + k) % R
+        pl.when(chip != r)(functools.partial(send_left, chip))
+        return carry
+
+    lax.fori_loop(1, R, send_left_rest, 0)
+    keep_left = pltpu.make_async_copy(lpack.at[pl.ds(q * CAP_L, CAP_L)], lland.at[left_spot], self_sem.at[4])
+    keep_left.start()
 
     def pack_right(d, carry):
         for k in range(CAP_R):
-            rpack[d * CAP_R + k] = panel[jnp.clip(lists[24 + d, k], 0, LANES - 1)]
+            rpack[d * CAP_R + k] = land[jnp.clip(lists[24 + d, k], 0, 2 * R * C - 1)]
         return carry
 
     lax.fori_loop(0, R, pack_right, 0)
+    right_spot = pl.ds(r * CAP_R, CAP_R)
 
     def send_right(rr):
-        src, dst = rpack.at[pl.ds(rr * CAP_R, CAP_R)], rland.at[pl.ds(r * CAP_R, CAP_R)]
-        remote(src, dst, xr_send, xr_recv, rr, c).start()
-
-    source = q == r
+        src = rpack.at[pl.ds(rr * CAP_R, CAP_R)]
+        remote(src, rland.at[right_spot], xr_send, xr_recv, rr, c).start()
+
     pl.when(jnp.logical_not(source))(functools.partial(send_right, q))
 
     def send_right_rest(k, carry):
@@ -315,14 +323,15 @@
         return carry
 
     lax.fori_loop(1, R, send_right_rest, 0)
-    keep_left = pltpu.make_async_copy(
-        lpack.at[pl.ds(c * CAP_L, CAP_L)], lland.at[pl.ds(c * CAP_L, CAP_L)], self_sem.at[4]
-    )
-    keep_right = pltpu.make_async_copy(
-        rpack.at[pl.ds(r * CAP_R, CAP_R)], rland.at[pl.ds(r * CAP_R, CAP_R)], self_sem.at[5]
-    )
-    keep_left.start()
+    keep_right = pltpu.make_async_copy(rpack.at[right_spot], rland.at[right_spot], self_sem.at[5])
     keep_right.start()
+
+    def collect(i, carry):
+        panel[i] = land[jnp.clip(lists[0, i], 0, 2 * R * C - 1)]
+        return carry
+
+    lax.fori_loop(0, LANES, collect, 0, unroll=8)
+
     save = pltpu.make_async_copy(panel, panel_out, out_sem)
     save.start()
 
@@ -353,9 +362,13 @@
     block_products(ta, tb, ot, True)
 
     keep_left.wait()
+    drain(lland.at[pl.ds(0, (R - 1) * CAP_L)], xl_recv)
+    left_half = lland.at[pl.ds(p * R * CAP_L, R * CAP_L)]
+    share = remote(left_half, left_half, yl_send, yl_recv, r, partner)
+    share.start()
     keep_right.wait()
-    drain(lland.at[pl.ds(0, (C - 1) * CAP_L)], xl_recv)
     drain(rland.at[pl.ds(0, (R - 1) * CAP_R)], xr_recv)
+    share.wait()
 
     def collect_pairs(i, carry):
         sorted_a[i] = lland[jnp.clip(lists[3, i], 0, C * CAP_L - 1)]
@@ -382,17 +395,33 @@
         )
         most = jnp.max(jnp.max(worst, axis=0, keepdims=True), axis=1, keepdims=True).astype(F32)
         told = jnp.where(lane1 < HALF, jnp.broadcast_to(partial, (1, LANES)), jnp.broadcast_to(most, (1, LANES)))
-        tr_src[...] = told
-        tr_land[c] = told
+        tr_row[p] = told
 
         def tell(k, carry):
-            d = (me + k) % (R * C)
-            remote(tr_src, tr_land.at[c], tr_send, tr_recv, d // C, d % C).start()
+            cc = (c + k) % C
+            remote(tr_row.at[p], tr_row.at[p], tr_send, tr_recv, r, cc).start()
             return carry
 
-        lax.fori_loop(1, R * C, tell, 0)
+        lax.fori_loop(1, C, tell, 0)
 
     block_products(ta, tc, tb, False)
+
+    @pl.when(source)
+    def _():
+        drain(tr_row.at[pl.ds(0, 1)], tr_recv)
+        drain(tr_all.at[pl.ds(0, C - 1)], tr_send)
+
+    @pl.when(jnp.logical_not(source))
+    def _():
+        drain(tr_row, tr_recv)
+
+    row_spot2 = pl.ds(2 * r, 2)
+
+    def pass_on(k, carry):
+        remote(tr_row, tr_all.at[row_spot2], tc_send, tc_recv, (r + k) % R, c).start()
+        return carry
+
+    lax.fori_loop(1, R, pass_on, 0)
     spread = onehot[...]
     for s in range(SUB):
         spot = slice(s * LANES, (s + 1) * LANES)
@@ -411,19 +440,13 @@
         spot = slice(s * LANES, (s + 1) * LANES)
         out[:, s, :] = jnp.transpose(ot[spot, :] * kept)
 
-    @pl.when(source)
-    def _():
-        drain(tr_land.at[pl.ds(0, C - 1)], tr_recv)
-        drain(tr_all, tr_send)
-
-    @pl.when(jnp.logical_not(source))
-    def _():
-        drain(tr_land, tr_recv)
-
-    trace, most = tr_land[0], tr_land[0]
+    drain(tr_all.at[pl.ds(0, 2 * (R - 1))], tc_recv)
+    drain(tr_all.at[pl.ds(0, 2 * (R - 1))], tc_send)
+    tr_all[row_spot2] = tr_row[...]
+    trace, most = tr_all[0], tr_all[0]
     for k in range(1, C):
-        trace = trace + tr_land[k]
-        most = jnp.maximum(most, tr_land[k])
+        trace = trace + tr_all[k]
+        most = jnp.maximum(most, tr_all[k])
     mean_out[...] = trace[:, 0:1] / (R * LANES)
     over_out[...] = most[:, HALF : HALF + 1]
 
@@ -433,7 +456,7 @@
     drain(land.at[pl.ds(0, 2 * (R * C - 1))], t1_send)
     drain(agr.at[pl.ds(0, 96)], ar_send)
     drain(dcol.at[pl.ds(0, 96)], ac_send)
-    drain(lland.at[pl.ds(0, (C - 1) * CAP_L)], xl_send)
+    drain(lland.at[pl.ds(0, (R - 1) * CAP_L)], xl_send)
     drain(rland.at[pl.ds(0, (R - 1) * CAP_R)], xr_send)
 
 
@@ -466,16 +489,15 @@
             pltpu.SMEM((32, LANES), I32),
             batch, batch, batch,
             wide, wide, wide, wide,
-            pltpu.VMEM((R * C - 1, 1, LANES), F32),
-            pltpu.VMEM((C * CAP_L,) + tile, F32),
+            pltpu.VMEM((R * CAP_L,) + tile, F32),
             pltpu.VMEM((R * CAP_R,) + tile, F32),
             pltpu.VMEM((C * CAP_L,) + tile, F32),
             pltpu.VMEM((R * CAP_R,) + tile, F32),
             pltpu.VMEM((LANES, LANES), BF16),
-            pltpu.VMEM((1, LANES), F32),
+            pltpu.VMEM((2, 1, LANES), F32),
             pltpu.VMEM((C, 1, LANES), F32),
             dma((SUB,)), dma((4 * R,)), dma((6,)), dma, dma,
-        ] + [dma] * 18,
+        ] + [dma] * 22,
         compiler_params=pltpu.CompilerParams(collective_id=0, has_side_effects=True),
     )(blocks, cols, slots, keep)
 

time: 59.7 us -> 57.8 us (0.968)
  Pallas kernels: 55.2 us -> 53.2 us
    pallas_call x1, Pallas kernels: 55.2 us -> 53.2 us  [sparse_product(): pl.pallas_call(kernel, out_shape=(jax.ShapeDtypeStruct((LANES,) + tile, F...]
where the time goes in v3:
time: 57.8 us; the launch traced here: 57.5 us
  Pallas kernels  53.2 us (92%)
  between operations  3.01 us (5%)
  local copies, waits for them, and re-layouts  1.27 us (2%)
    pallas_call x1, Pallas kernels, sparse_product(): pl.pallas_call(kernel, out_shape=(jax.ShapeDtypeStruct((LANES,) + tile, F...  53.2 us

profile of v3, /device:TPU:1, one launch (start us, length us, event | category | flops | bytes accessed | tf_op | source)
XLA Modules:
  0.0 57.5 jit_solution(110959657364593682)
XLA Ops:
  0.6 53.2 %shard_map.59 = (f32[128,8,128]{2,1,0:T(8,128)S(1)}, f32[1,1]{1,0:T(1,128)}, f32[1,1]{1,0:T(1,128)}, f32[128,8,128]{2,1,0:T(8,128)S(1)}) custom-call(f32[16,16,1024]{2,1,0:T(8,128)} %blocks.1, s32[16,1024]{1,0:T(8,128)} %bitcast.46, s32[8,128]{1,0:T(8,128)} %bitcast.47, s32[1,128]{1,0:T(1,128)} %bitcast.48), custom_call_target="tpu_custom_call" | custom-call | tf_op jit(solution)/shard_map/pallas_call | solution.py:470
  54.5 1.3 %conditional.1 = (f32[1,1]{1,0:T(1,128)}, f32[128,1,1024]{2,1,0:T(1,128)}) conditional(s32[]{:T(128)} %bitcast.11, (f32[1,1]{1,0:T(1,128)}, f32[128,8,128]{2,1,0:T(8,128)S(1)}) %tuple.70, (s32[1024,16]{0,1:T(8,128)}, f32[128,8,128]{2,1,0:T(8,128)S(1)}, s32[128,1]{0,1:T(1,128)}) %tuple.71), branch_computations={%region_0.0_spmd, %region_1.12_spmd} | conditional | flops 51123376 | bytes 26870564 | solution.py:552
  54.6 0.2 copy.13
  54.8 1.0 %copy.16 = f32[128,1,1024]{2,1,0:T(1,128)} copy(f32[128,1,1024]{0,2,1:T(8,128)S(1)} %bitcast.45) | data formatting | bytes 1048576 | tf_op jit(solution)/shard_map/cond

commit v4 on v3

--- a/solution.py
+++ b/solution.py
@@ -60,7 +60,7 @@
     blocks, cols, slots, keep,
     out, mean_out, over_out, panel_out,
     xv, land, agr, dcol, ctb, ct3, tt, lists_v, lists,
-    panel, sorted_a, sorted_b, ta, tb, tc, ot,
+    panel, sorted_a, sorted_b, pair_a, pair_b, ta, tb, tc, pa, pb, ot,
     lpack, rpack, lland, rland, onehot, tr_row, tr_all,
     in_sem, ct_sem, self_sem, list_sem, out_sem,
     sr_send, sc_send, sr_recv, sc_recv,
@@ -285,14 +285,27 @@
         return carry
 
     lax.fori_loop(0, R, pack_left, 0)
+    def pack_right(d, carry):
+        for k in range(CAP_R):
+            rpack[d * CAP_R + k] = land[jnp.clip(lists[24 + d, k], 0, 2 * R * C - 1)]
+        return carry
+
+    lax.fori_loop(0, R, pack_right, 0)
     left_spot = pl.ds((p * R + q) * CAP_L, CAP_L)
 
     def send_left(chip):
         src = lpack.at[pl.ds(chip * CAP_L, CAP_L)]
         remote(src, lland.at[left_spot], xl_send, xl_recv, r, 2 * chip + p).start()
 
+    right_spot = pl.ds(r * CAP_R, CAP_R)
+
+    def send_right(rr):
+        src = rpack.at[pl.ds(rr * CAP_R, CAP_R)]
+        remote(src, rland.at[right_spot], xr_send, xr_recv, rr, c).start()
+
     source = q == r
     pl.when(jnp.logical_not(source))(functools.partial(send_left, r))
+    pl.when(jnp.logical_not(source))(functools.partial(send_right, q))
 
     def send_left_rest(k, carry):
         chip = (q + k) % R
@@ -303,20 +316,6 @@
     keep_left = pltpu.make_async_copy(lpack.at[pl.ds(q * CAP_L, CAP_L)], lland.at[left_spot], self_sem.at[4])
     keep_left.start()
 
-    def pack_right(d, carry):
-        for k in range(CAP_R):
-            rpack[d * CAP_R + k] = land[jnp.clip(lists[24 + d, k], 0, 2 * R * C - 1)]
-        return carry
-
-    lax.fori_loop(0, R, pack_right, 0)
-    right_spot = pl.ds(r * CAP_R, CAP_R)
-
-    def send_right(rr):
-        src = rpack.at[pl.ds(rr * CAP_R, CAP_R)]
-        remote(src, rland.at[right_spot], xr_send, xr_recv, rr, c).start()
-
-    pl.when(jnp.logical_not(source))(functools.partial(send_right, q))
-
     def send_right_rest(k, carry):
         rr = (r + k) % R
         pl.when(rr != q)(functools.partial(send_right, rr))
@@ -340,53 +339,36 @@
     forward.start()
 
     to_lanes(panel, tb)
-    drain(dcol.at[pl.ds(0, 96)], ac_recv)
-
-    def collect_column(i, carry):
-        sorted_b[i] = dcol[jnp.clip(lists[2, i], 0, R * C - 1)]
-        return carry
-
-    lax.fori_loop(0, LANES, collect_column, 0, unroll=8)
-    to_lanes(sorted_b, tc)
-    block_products(tb, tc, ot, False)
-    forward.wait()
-
-    def collect_row(i, carry):
-        sorted_a[i] = agr[jnp.clip(lists[1, i], 0, 2 * R * C - 1)]
-        return carry
-
-    lax.fori_loop(0, LANES, collect_row, 0, unroll=8)
     lane1 = iota((1, LANES), 1)
     group1 = 2 * r + lane1 // HALF
-    to_lanes(sorted_a, ta, (group1 != c).astype(F32))
-    block_products(ta, tb, ot, True)
-
-    keep_left.wait()
-    drain(lland.at[pl.ds(0, (R - 1) * CAP_L)], xl_recv)
-    left_half = lland.at[pl.ds(p * R * CAP_L, R * CAP_L)]
-    share = remote(left_half, left_half, yl_send, yl_recv, r, partner)
-    share.start()
-    keep_right.wait()
-    drain(rland.at[pl.ds(0, (R - 1) * CAP_R)], xr_recv)
-    share.wait()
-
-    def collect_pairs(i, carry):
-        sorted_a[i] = lland[jnp.clip(lists[3, i], 0, C * CAP_L - 1)]
-        sorted_b[i] = rland[jnp.clip(lists[4, i], 0, R * CAP_R - 1)]
-        return carry
-
-    lax.fori_loop(0, LANES, collect_pairs, 0, unroll=8)
-    to_lanes(sorted_a, ta)
-    to_lanes(sorted_b, tc)
+
+    def receive_pairs():
+        keep_left.wait()
+        drain(lland.at[pl.ds(0, (R - 1) * CAP_L)], xl_recv)
+        left_half = lland.at[pl.ds(p * R * CAP_L, R * CAP_L)]
+        share = remote(left_half, left_half, yl_send, yl_recv, r, partner)
+        share.start()
+        keep_right.wait()
+        drain(rland.at[pl.ds(0, (R - 1) * CAP_R)], xr_recv)
+        share.wait()
+
+        def collect_pairs(i, carry):
+            pair_a[i] = lland[jnp.clip(lists[3, i], 0, C * CAP_L - 1)]
+            pair_b[i] = rland[jnp.clip(lists[4, i], 0, R * CAP_R - 1)]
+            return carry
+
+        lax.fori_loop(0, LANES, collect_pairs, 0, unroll=8)
+        to_lanes(pair_a, pa)
+        to_lanes(pair_b, pb)
 
     @pl.when(source)
     def _():
-        diagonal = ot[0:1, :]
-        for x in range(1, BS):
-            diagonal = diagonal + ot[33 * x : 33 * x + 1, :]
-        totals = jnp.zeros((BS, LANES), F32)
+        receive_pairs()
+        own_terms, totals = jnp.zeros((BS, LANES), F32), jnp.zeros((BS, LANES), F32)
         for x in range(BS):
-            totals = totals + ta[BS * x : BS * (x + 1), :] * tc[pl.ds(x, BS, stride=BS), :]
+            own_terms = own_terms + tb[BS * x : BS * (x + 1), :] * tb[pl.ds(x, BS, stride=BS), :]
+            totals = totals + pa[BS * x : BS * (x + 1), :] * pb[pl.ds(x, BS, stride=BS), :]
+        diagonal = jnp.sum(own_terms, axis=0, keepdims=True)
         pairs = jnp.sum(totals, axis=0, keepdims=True)
         inside = jnp.broadcast_to((group1 == c).astype(BF16), (8, LANES))
         weight = lax.dot_general(inside, onehot[...], (((1,), (1,)), ((), ())), preferred_element_type=F32)
@@ -404,7 +386,24 @@
 
         lax.fori_loop(1, C, tell, 0)
 
-    block_products(ta, tc, tb, False)
+    drain(dcol.at[pl.ds(0, 96)], ac_recv)
+
+    def collect_column(i, carry):
+        sorted_b[i] = dcol[jnp.clip(lists[2, i], 0, R * C - 1)]
+        return carry
+
+    lax.fori_loop(0, LANES, collect_column, 0, unroll=8)
+    to_lanes(sorted_b, tc)
+    block_products(tb, tc, ot, False)
+    forward.wait()
+
+    def collect_row(i, carry):
+        sorted_a[i] = agr[jnp.clip(lists[1, i], 0, 2 * R * C - 1)]
+        return carry
+
+    lax.fori_loop(0, LANES, collect_row, 0, unroll=8)
+    to_lanes(sorted_a, ta, (group1 != c).astype(F32))
+    block_products(ta, tb, ot, True)
 
     @pl.when(source)
     def _():
@@ -422,6 +421,11 @@
         return carry
 
     lax.fori_loop(1, R, pass_on, 0)
+
+    pl.when(jnp.logical_not(source))(receive_pairs)
+
+    block_products(pa, pb, tb, False)
+
     spread = onehot[...]
     for s in range(SUB):
         spot = slice(s * LANES, (s + 1) * LANES)
@@ -487,8 +491,8 @@
             pltpu.VMEM((C, C, LANES), I32),
             pltpu.VMEM((32, LANES), I32),
             pltpu.SMEM((32, LANES), I32),
-            batch, batch, batch,
-            wide, wide, wide, wide,
+            batch, batch, batch, batch, batch,
+            wide, wide, wide, wide, wide, wide,
             pltpu.VMEM((R * CAP_L,) + tile, F32),
             pltpu.VMEM((R * CAP_R,) + tile, F32),
             pltpu.VMEM((C * CAP_L,) + tile, F32),
@@ -543,7 +547,8 @@
             return total + moving, moving
         trace, _ = lax.fori_loop(1, lax.axis_size(axis), add, (trace, trace))
     filtered = totals.reshape(LANES, AREA) * keep.reshape(LANES, 1).astype(F32)
-    return filtered.reshape(LANES, SUB, LANES), trace[0, 0] / (R * LANES)
+    filtered = lax.optimization_barrier(filtered.reshape(SUB * LANES, LANES))
+    return filtered, trace[0, 0] / (R * LANES)
 
 
 def shards(blocks, columns, owner_slot, keep_mask):
@@ -553,8 +558,9 @@
         over.reshape(()) > 0,
         lambda f, t, s: dense_product(s, columns, keep),
         lambda f, t, s: (f, t),
-        filtered, mean.reshape(()), panel,
+        filtered.reshape(SUB * LANES, LANES), mean.reshape(()), panel,
     )
+    filtered = lax.optimization_barrier(filtered)
     return filtered.reshape(LANES, 1, AREA), mean
 
 

time: 57.8 us -> 57.5 us (level)
    cond x1 -> x0, local copies, waits for them, and re-layouts: 1.04 us -> none
    unnamed x0 -> x1, local copies, waits for them, and re-layouts: none -> 0.8 us
where the time goes in v4:
time: 57.5 us; the launch traced here: 57.1 us
  Pallas kernels  53.1 us (92%)
  between operations  3.02 us (5%)
  local copies, waits for them, and re-layouts  0.8 us (1%)
    pallas_call x1, Pallas kernels, sparse_product(): pl.pallas_call(kernel, out_shape=(jax.ShapeDtypeStruct((LANES,) + tile, F...  53.1 us

profile of v4, /device:TPU:1, one launch (start us, length us, event | category | flops | bytes accessed | tf_op | source)
XLA Modules:
  0.0 57.1 jit_solution(3357405583058466920)
XLA Ops:
  0.6 53.1 %shard_map.59 = (f32[128,8,128]{2,1,0:T(8,128)S(1)}, f32[1,1]{1,0:T(1,128)}, f32[1,1]{1,0:T(1,128)}, f32[128,8,128]{2,1,0:T(8,128)S(1)}) custom-call(f32[16,16,1024]{2,1,0:T(8,128)} %blocks.1, s32[16,1024]{1,0:T(8,128)} %bitcast.44, s32[8,128]{1,0:T(8,128)} %bitcast.45, s32[1,128]{1,0:T(1,128)} %bitcast.46), custom_call_target="tpu_custom_call" | custom-call | tf_op jit(solution)/shard_map/pallas_call | solution.py:474
  54.5 0.2 conditional.1
  54.6 0.8 %copy.65 = f32[128,1,1024]{2,1,0:T(1,128)} copy(f32[128,1,1024]{2,1,0:T(1,128)S(1)} %bitcast.43) | data formatting | bytes 1048576

commit v5 on v4

--- a/solution.py
+++ b/solution.py
@@ -361,6 +361,25 @@
         to_lanes(pair_a, pa)
         to_lanes(pair_b, pb)
 
+    drain(dcol.at[pl.ds(0, 96)], ac_recv)
+
+    def collect_column(i, carry):
+        sorted_b[i] = dcol[jnp.clip(lists[2, i], 0, R * C - 1)]
+        return carry
+
+    lax.fori_loop(0, LANES, collect_column, 0, unroll=8)
+    to_lanes(sorted_b, tc)
+    block_products(tb, tc, ot, False)
+    forward.wait()
+
+    def collect_row(i, carry):
+        sorted_a[i] = agr[jnp.clip(lists[1, i], 0, 2 * R * C - 1)]
+        return carry
+
+    lax.fori_loop(0, LANES, collect_row, 0, unroll=8)
+    to_lanes(sorted_a, ta, (group1 != c).astype(F32))
+    block_products(ta, tb, ot, True)
+
     @pl.when(source)
     def _():
         receive_pairs()
@@ -386,24 +405,9 @@
 
         lax.fori_loop(1, C, tell, 0)
 
-    drain(dcol.at[pl.ds(0, 96)], ac_recv)
-
-    def collect_column(i, carry):
-        sorted_b[i] = dcol[jnp.clip(lists[2, i], 0, R * C - 1)]
-        return carry
-
-    lax.fori_loop(0, LANES, collect_column, 0, unroll=8)
-    to_lanes(sorted_b, tc)
-    block_products(tb, tc, ot, False)
-    forward.wait()
-
-    def collect_row(i, carry):
-        sorted_a[i] = agr[jnp.clip(lists[1, i], 0, 2 * R * C - 1)]
-        return carry
-
-    lax.fori_loop(0, LANES, collect_row, 0, unroll=8)
-    to_lanes(sorted_a, ta, (group1 != c).astype(F32))
-    block_products(ta, tb, ot, True)
+    pl.when(jnp.logical_not(source))(receive_pairs)
+
+    block_products(pa, pb, tb, False)
 
     @pl.when(source)
     def _():
@@ -422,9 +426,6 @@
 
     lax.fori_loop(1, R, pass_on, 0)
 
-    pl.when(jnp.logical_not(source))(receive_pairs)
-
-    block_products(pa, pb, tb, False)
 
     spread = onehot[...]
     for s in range(SUB):

time: 57.5 us -> 57.9 us (level)
  Pallas kernels: 53.1 us -> 53.7 us
where the time goes in v5:
time: 57.9 us; the launch traced here: 57.7 us
  Pallas kernels  53.7 us (93%)
  between operations  3.02 us (5%)
  local copies, waits for them, and re-layouts  0.8 us (1%)
    pallas_call x1, Pallas kernels, sparse_product(): pl.pallas_call(kernel, out_shape=(jax.ShapeDtypeStruct((LANES,) + tile, F...  53.7 us

profile of v5, /device:TPU:1, one launch (start us, length us, event | category | flops | bytes accessed | tf_op | source)
XLA Modules:
  0.0 57.7 jit_solution(6668682792397159271)
XLA Ops:
  0.6 53.7 %shard_map.59 = (f32[128,8,128]{2,1,0:T(8,128)S(1)}, f32[1,1]{1,0:T(1,128)}, f32[1,1]{1,0:T(1,128)}, f32[128,8,128]{2,1,0:T(8,128)S(1)}) custom-call(f32[16,16,1024]{2,1,0:T(8,128)} %blocks.1, s32[16,1024]{1,0:T(8,128)} %bitcast.44, s32[8,128]{1,0:T(8,128)} %bitcast.45, s32[1,128]{1,0:T(1,128)} %bitcast.46), custom_call_target="tpu_custom_call" | custom-call | tf_op jit(solution)/shard_map/pallas_call | solution.py:475
  55.0 0.2 conditional.1
  55.2 0.8 %copy.65 = f32[128,1,1024]{2,1,0:T(1,128)} copy(f32[128,1,1024]{2,1,0:T(1,128)S(1)} %bitcast.43) | data formatting | bytes 1048576

commit v6 on v4

--- a/solution.py
+++ b/solution.py
@@ -14,6 +14,7 @@
 HALF = 64
 CAP_L = 16
 CAP_R = 16
+CAP_T = 8
 MESH = pl.DeviceIdType.MESH
 F32, I32, BF16 = jnp.float32, jnp.int32, jnp.bfloat16
 HIGHEST = lax.Precision.HIGHEST
@@ -61,11 +62,11 @@
     out, mean_out, over_out, panel_out,
     xv, land, agr, dcol, ctb, ct3, tt, lists_v, lists,
     panel, sorted_a, sorted_b, pair_a, pair_b, ta, tb, tc, pa, pb, ot,
-    lpack, rpack, lland, rland, onehot, tr_row, tr_all,
+    lpack, rpack, lland, rland, onehot, mpack, mland, tr_all,
     in_sem, ct_sem, self_sem, list_sem, out_sem,
     sr_send, sc_send, sr_recv, sc_recv,
     t1_send, t1_recv, ar_send, ac_send, ar_recv, ac_recv, fw_send, fw_recv,
-    xl_send, xr_send, xl_recv, xr_recv, yl_send, yl_recv, tr_send, tr_recv, tc_send, tc_recv,
+    xl_send, xr_send, xl_recv, xr_recv, yl_send, yl_recv, tr_send, tr_recv, tc_send, tc_recv, m_send, m_recv,
 ):
     r = lax.axis_index("row")
     c = lax.axis_index("col")
@@ -202,6 +203,29 @@
         )
         right_list = jnp.where(lane8 == k, value, right_list)
     lists_v[24:32, :] = right_list
+    mutual_send, mutual_take, mutual_count = [], [], []
+    for h in range(2):
+        g = 2 * r + h
+        own_place = jnp.broadcast_to(ct3[c, pl.ds(r, 1), :] % LANES, (8, LANES))
+        back = lookup(jnp.broadcast_to(ct3[g, pl.ds(q, 1), :], (8, LANES)), own_place)
+        ours = (back == LANES * r + lane8) & (half == h) & (c != g)
+        ours_rank = count_before(ours)
+        their_place = jnp.broadcast_to(ct3[g, pl.ds(q, 1), :] % LANES, (8, LANES))
+        back = lookup(jnp.broadcast_to(ct3[c, pl.ds(r, 1), :], (8, LANES)), their_place)
+        theirs = (back == LANES * q + lane8) & (half == p) & (c != g)
+        theirs_rank = count_before(theirs)
+        theirs_land = lookup(at_land, their_place)
+        send_list, take_list = jnp.zeros((8, LANES), I32), jnp.zeros((8, LANES), I32)
+        for k in range(CAP_T):
+            value = jnp.sum(jnp.where(ours & (ours_rank == k), at_land, 0), axis=1, keepdims=True)
+            send_list = jnp.where(lane8 == k, value, send_list)
+            value = jnp.sum(jnp.where(theirs & (theirs_rank == k), theirs_land, 0), axis=1, keepdims=True)
+            take_list = jnp.where(lane8 == k, value, take_list)
+        mutual_send.append(send_list)
+        mutual_take.append(take_list)
+        mutual_count.append(jnp.broadcast_to(count(theirs), (8, LANES)))
+    mutual = jnp.where(sub8 == 0, mutual_send[0], jnp.where(sub8 == 1, mutual_send[1], mutual_take[0]))
+    lists_v[32:40, :] = jnp.where(sub8 == 3, mutual_take[1], mutual)
     to_smem = pltpu.make_async_copy(lists_v, lists, list_sem)
     to_smem.start()
 
@@ -279,6 +303,18 @@
     to_smem.wait()
     drain(land.at[pl.ds(0, 2 * (R * C - 1))], t1_recv)
 
+    for h in range(2):
+        for k in range(CAP_T):
+            mpack[h * CAP_T + k] = land[jnp.clip(lists[32 + h, k], 0, 2 * R * C - 1)]
+    diagonal_chip = q == r
+    mine_spot = pl.ds(p * CAP_T, CAP_T)
+
+    def send_mutual(h):
+        remote(mpack.at[pl.ds(h * CAP_T, CAP_T)], mland.at[mine_spot], m_send, m_recv, q, 2 * r + h).start()
+
+    for h in range(2):
+        pl.when(jnp.logical_not(diagonal_chip & (p == h)))(functools.partial(send_mutual, h))
+
     def pack_left(d, carry):
         for k in range(CAP_L):
             lpack[d * CAP_L + k] = land[jnp.clip(lists[8 + 2 * d, k], 0, 2 * R * C - 1)]
@@ -303,13 +339,9 @@
         src = rpack.at[pl.ds(rr * CAP_R, CAP_R)]
         remote(src, rland.at[right_spot], xr_send, xr_recv, rr, c).start()
 
-    source = q == r
-    pl.when(jnp.logical_not(source))(functools.partial(send_left, r))
-    pl.when(jnp.logical_not(source))(functools.partial(send_right, q))
 
     def send_left_rest(k, carry):
-        chip = (q + k) % R
-        pl.when(chip != r)(functools.partial(send_left, chip))
+        send_left((q + k) % R)
         return carry
 
     lax.fori_loop(1, R, send_left_rest, 0)
@@ -317,8 +349,7 @@
     keep_left.start()
 
     def send_right_rest(k, carry):
-        rr = (r + k) % R
-        pl.when(rr != q)(functools.partial(send_right, rr))
+        send_right((r + k) % R)
         return carry
 
     lax.fori_loop(1, R, send_right_rest, 0)
@@ -361,31 +392,6 @@
         to_lanes(pair_a, pa)
         to_lanes(pair_b, pb)
 
-    @pl.when(source)
-    def _():
-        receive_pairs()
-        own_terms, totals = jnp.zeros((BS, LANES), F32), jnp.zeros((BS, LANES), F32)
-        for x in range(BS):
-            own_terms = own_terms + tb[BS * x : BS * (x + 1), :] * tb[pl.ds(x, BS, stride=BS), :]
-            totals = totals + pa[BS * x : BS * (x + 1), :] * pb[pl.ds(x, BS, stride=BS), :]
-        diagonal = jnp.sum(own_terms, axis=0, keepdims=True)
-        pairs = jnp.sum(totals, axis=0, keepdims=True)
-        inside = jnp.broadcast_to((group1 == c).astype(BF16), (8, LANES))
-        weight = lax.dot_general(inside, onehot[...], (((1,), (1,)), ((), ())), preferred_element_type=F32)
-        partial = jnp.sum(
-            jnp.where(group1 == c, diagonal, 0.0) + pairs * weight[0:1, :], axis=1, keepdims=True
-        )
-        most = jnp.max(jnp.max(worst, axis=0, keepdims=True), axis=1, keepdims=True).astype(F32)
-        told = jnp.where(lane1 < HALF, jnp.broadcast_to(partial, (1, LANES)), jnp.broadcast_to(most, (1, LANES)))
-        tr_row[p] = told
-
-        def tell(k, carry):
-            cc = (c + k) % C
-            remote(tr_row.at[p], tr_row.at[p], tr_send, tr_recv, r, cc).start()
-            return carry
-
-        lax.fori_loop(1, C, tell, 0)
-
     drain(dcol.at[pl.ds(0, 96)], ac_recv)
 
     def collect_column(i, carry):
@@ -395,6 +401,39 @@
     lax.fori_loop(0, LANES, collect_column, 0, unroll=8)
     to_lanes(sorted_b, tc)
     block_products(tb, tc, ot, False)
+    @pl.when(diagonal_chip)
+    def _():
+        drain(mland.at[pl.ds(0, CAP_T)], m_recv)
+
+    @pl.when(jnp.logical_not(diagonal_chip))
+    def _():
+        drain(mland, m_recv)
+
+    for t in range(2):
+        for k in range(CAP_T):
+            pair_a[t * CAP_T + k] = mland[t * CAP_T + k]
+            pair_b[t * CAP_T + k] = land[jnp.clip(lists[34 + t, k], 0, 2 * R * C - 1)]
+    to_lanes(pair_a, pa)
+    to_lanes(pair_b, pb)
+    own_terms, totals = jnp.zeros((BS, LANES), F32), jnp.zeros((BS, LANES), F32)
+    for x in range(BS):
+        own_terms = own_terms + tb[BS * x : BS * (x + 1), :] * tb[pl.ds(x, BS, stride=BS), :]
+        totals = totals + pa[BS * x : BS * (x + 1), :] * pb[pl.ds(x, BS, stride=BS), :]
+    squares = jnp.where(group1 == c, jnp.sum(own_terms, axis=0, keepdims=True), 0.0)
+    filled = jnp.where(lane1 < CAP_T, mutual_count[0][0:1, :], mutual_count[1][0:1, :] + CAP_T)
+    filled = (lane1 < filled) & (lane1 < 2 * CAP_T)
+    pairs = jnp.where(filled, jnp.sum(totals, axis=0, keepdims=True), 0.0)
+    partial = jnp.broadcast_to(jnp.sum(squares + pairs, axis=1, keepdims=True), (1, LANES))
+    most = jnp.max(jnp.max(worst, axis=0, keepdims=True), axis=1, keepdims=True)
+    most = jnp.maximum(jnp.broadcast_to(most, (1, LANES)), jnp.maximum(mutual_count[0], mutual_count[1])[0:1, :] - CAP_T)
+    tr_all[me] = jnp.where(lane1 < HALF, partial, most.astype(F32))
+
+    def tell(k, carry):
+        remote(tr_all.at[me], tr_all.at[me], tr_send, tr_recv, r, (c + k) % C).start()
+        return carry
+
+    lax.fori_loop(1, C, tell, 0)
+
     forward.wait()
 
     def collect_row(i, carry):
@@ -405,25 +444,16 @@
     to_lanes(sorted_a, ta, (group1 != c).astype(F32))
     block_products(ta, tb, ot, True)
 
-    @pl.when(source)
-    def _():
-        drain(tr_row.at[pl.ds(0, 1)], tr_recv)
-        drain(tr_all.at[pl.ds(0, C - 1)], tr_send)
-
-    @pl.when(jnp.logical_not(source))
-    def _():
-        drain(tr_row, tr_recv)
-
-    row_spot2 = pl.ds(2 * r, 2)
+    drain(tr_all.at[pl.ds(0, C - 1)], tr_recv)
+    row_tiles = tr_all.at[pl.ds(C * r, C)]
 
     def pass_on(k, carry):
-        remote(tr_row, tr_all.at[row_spot2], tc_send, tc_recv, (r + k) % R, c).start()
+        remote(row_tiles, row_tiles, tc_send, tc_recv, (r + k) % R, c).start()
         return carry
 
     lax.fori_loop(1, R, pass_on, 0)
 
-    pl.when(jnp.logical_not(source))(receive_pairs)
-
+    receive_pairs()
     block_products(pa, pb, tb, False)
 
     spread = onehot[...]
@@ -444,16 +474,21 @@
         spot = slice(s * LANES, (s + 1) * LANES)
         out[:, s, :] = jnp.transpose(ot[spot, :] * kept)
 
-    drain(tr_all.at[pl.ds(0, 2 * (R - 1))], tc_recv)
-    drain(tr_all.at[pl.ds(0, 2 * (R - 1))], tc_send)
-    tr_all[row_spot2] = tr_row[...]
-    trace, most = tr_all[0], tr_all[0]
-    for k in range(1, C):
-        trace = trace + tr_all[k]
-        most = jnp.maximum(most, tr_all[k])
-    mean_out[...] = trace[:, 0:1] / (R * LANES)
-    over_out[...] = most[:, HALF : HALF + 1]
-
+    drain(tr_all.at[pl.ds(0, C * (R - 1))], tc_recv)
+    tiles = tr_all[...]
+    mean_out[...] = jnp.sum(tiles, axis=0)[:, 0:1] / (R * LANES)
+    over_out[...] = jnp.max(tiles, axis=0)[:, HALF : HALF + 1]
+
+    @pl.when(diagonal_chip)
+    def _():
+        drain(mland.at[pl.ds(0, CAP_T)], m_send)
+
+    @pl.when(jnp.logical_not(diagonal_chip))
+    def _():
+        drain(mland, m_send)
+
+    drain(tr_all.at[pl.ds(0, C - 1)], tr_send)
+    drain(tr_all.at[pl.ds(0, C * (R - 1))], tc_send)
     save.wait()
     drain(agr.at[pl.ds(0, 30)], sr_send)
     drain(dcol.at[pl.ds(0, 31)], sc_send)
@@ -489,8 +524,8 @@
             pltpu.VMEM((R, C, LANES), I32),
             pltpu.VMEM((C, R, LANES), I32),
             pltpu.VMEM((C, C, LANES), I32),
-            pltpu.VMEM((32, LANES), I32),
-            pltpu.SMEM((32, LANES), I32),
+            pltpu.VMEM((40, LANES), I32),
+            pltpu.SMEM((40, LANES), I32),
             batch, batch, batch, batch, batch,
             wide, wide, wide, wide, wide, wide,
             pltpu.VMEM((R * CAP_L,) + tile, F32),
@@ -498,10 +533,11 @@
             pltpu.VMEM((C * CAP_L,) + tile, F32),
             pltpu.VMEM((R * CAP_R,) + tile, F32),
             pltpu.VMEM((LANES, LANES), BF16),
-            pltpu.VMEM((2, 1, LANES), F32),
-            pltpu.VMEM((C, 1, LANES), F32),
+            pltpu.VMEM((2 * CAP_T,) + tile, F32),
+            pltpu.VMEM((2 * CAP_T,) + tile, F32),
+            pltpu.VMEM((R * C, 1, LANES), F32),
             dma((SUB,)), dma((4 * R,)), dma((6,)), dma, dma,
-        ] + [dma] * 22,
+        ] + [dma] * 24,
         compiler_params=pltpu.CompilerParams(collective_id=0, has_side_effects=True),
     )(blocks, cols, slots, keep)
 

time: 57.5 us -> 60.7 us (1.056)
  Pallas kernels: 53.1 us -> 56.3 us
    pallas_call x1, Pallas kernels: 53.1 us -> 56.3 us  [sparse_product(): pl.pallas_call(kernel, out_shape=(jax.ShapeDtypeStruct((LANES,) + tile, F...]
where the time goes in v6:
time: 60.7 us; the launch traced here: 60.3 us
  Pallas kernels  56.3 us (93%)
  between operations  3.02 us (5%)
  local copies, waits for them, and re-layouts  0.8 us (1%)
    pallas_call x1, Pallas kernels, sparse_product(): pl.pallas_call(kernel, out_shape=(jax.ShapeDtypeStruct((LANES,) + tile, F...  56.3 us

profile of v6, /device:TPU:1, one launch (start us, length us, event | category | flops | bytes accessed | tf_op | source)
XLA Modules:
  0.0 60.3 jit_solution(8385835852671595446)
XLA Ops:
  0.6 56.3 %shard_map.59 = (f32[128,8,128]{2,1,0:T(8,128)S(1)}, f32[1,1]{1,0:T(1,128)}, f32[1,1]{1,0:T(1,128)}, f32[128,8,128]{2,1,0:T(8,128)S(1)}) custom-call(f32[16,16,1024]{2,1,0:T(8,128)} %blocks.1, s32[16,1024]{1,0:T(8,128)} %bitcast.44, s32[8,128]{1,0:T(8,128)} %bitcast.45, s32[1,128]{1,0:T(1,128)} %bitcast.46), custom_call_target="tpu_custom_call" | custom-call | tf_op jit(solution)/shard_map/pallas_call | solution.py:509
  57.6 0.2 conditional.1
  57.8 0.8 %copy.65 = f32[128,1,1024]{2,1,0:T(1,128)} copy(f32[128,1,1024]{2,1,0:T(1,128)S(1)} %bitcast.43) | data formatting | bytes 1048576

commit v7 on v4

--- a/solution.py
+++ b/solution.py
@@ -234,7 +234,7 @@
         remote(xv.at[pl.ds(2 * rr, 2), cc], land.at[pl.ds(2 * me, 2)], t1_send, t1_recv, rr, cc).start()
         return carry
 
-    lax.fori_loop(1, R * C, exchange, 0)
+    lax.fori_loop(1, 64, exchange, 0)
     own = [
         pltpu.make_async_copy(xv.at[2 * r, 2 * r], agr.at[row_spot], self_sem.at[0]),
         pltpu.make_async_copy(xv.at[2 * r + 1, 2 * r + 1], agr.at[row_spot + 1], self_sem.at[1]),
@@ -263,6 +263,8 @@
         return carry
 
     lax.fori_loop(1, 4, col_gather, 0)
+
+    lax.fori_loop(64, R * C, exchange, 0)
 
     even = sub16 % 2 == 0
     worst = jnp.full((C, LANES), -1, I32)

time: 57.5 us -> 67.4 us (1.17)
  Pallas kernels: 53.1 us -> 63 us
    pallas_call x1, Pallas kernels: 53.1 us -> 63 us  [sparse_product(): pl.pallas_call(kernel, out_shape=(jax.ShapeDtypeStruct((LANES,) + tile, F...]
where the time goes in v7:
time: 67.4 us; the launch traced here: 67 us
  Pallas kernels  63 us (93%)
  between operations  3.02 us (4%)
  local copies, waits for them, and re-layouts  0.8 us (1%)
    pallas_call x1, Pallas kernels, sparse_product(): pl.pallas_call(kernel, out_shape=(jax.ShapeDtypeStruct((LANES,) + tile, F...  63 us

profile of v7, /device:TPU:1, one launch (start us, length us, event | category | flops | bytes accessed | tf_op | source)
XLA Modules:
  0.0 67.0 jit_solution(11572966069006426649)
XLA Ops:
  0.6 63.0 %shard_map.59 = (f32[128,8,128]{2,1,0:T(8,128)S(1)}, f32[1,1]{1,0:T(1,128)}, f32[1,1]{1,0:T(1,128)}, f32[128,8,128]{2,1,0:T(8,128)S(1)}) custom-call(f32[16,16,1024]{2,1,0:T(8,128)} %blocks.1, s32[16,1024]{1,0:T(8,128)} %bitcast.44, s32[8,128]{1,0:T(8,128)} %bitcast.45, s32[1,128]{1,0:T(1,128)} %bitcast.46), custom_call_target="tpu_custom_call" | custom-call | tf_op jit(solution)/shard_map/pallas_call | solution.py:476
  64.4 0.2 conditional.1
  64.6 0.8 %copy.65 = f32[128,1,1024]{2,1,0:T(1,128)} copy(f32[128,1,1024]{2,1,0:T(1,128)S(1)} %bitcast.43) | data formatting | bytes 1048576
